TPU v7x, 32 devices: a whole 2x2x4 slice. The times are simulated.
32 devices in a mesh: dp: 8 (over y, x, core), tensor: 4 (over z).
Axes of the slice: x: 2, y: 2, z: 4, core: 2. Of those that a mesh axis runs over, the one named last changes fastest.
Arguments:
- tokens: bfloat16 [16384, 1024], P(('dp', 'tensor')), may hold values from -6 to 6
- norm_gains: float32 [2, 1024], replicated, may hold values from 0.5 to 1.5
- attn_qkv: bfloat16 [3, 1024, 1024], P(None, None, 'tensor'), may hold values from -0.09375 to 0.09375
- attn_out: bfloat16 [1024, 1024], P('tensor'), may hold values from -1.5 to 1.5
- ffn_in: bfloat16 [2, 1024, 2816], P(None, None, 'tensor'), may hold values from -0.1875 to 0.1875
- ffn_out: bfloat16 [2816, 1024], P('tensor'), may hold values from -0.109375 to 0.109375
- position_tables: float32 [3, 32, 16], P(None, None, 'tensor'), may hold values from -5 to 5
- page_counts: int32 [16], P('dp'), may hold values from 64 to 1024, as said below
- layout_cells: int32 [2, 16384], P(None, 'dp'), may hold values from 0 to 63
- cotangent: bfloat16 [16384, 1024], P(('dp', 'tensor')), may hold values from -6 to 6
Outputs:
- layer_out: bfloat16 [16384, 1024], P(('dp', 'tensor'))
- tokens_grad: float32 [16384, 1024], P(('dp', 'tensor'))
- gains_grad: float32 [2, 1024], P(None, ('dp', 'tensor'))
- qkv_grad: float32 [3, 1024, 1024], P(None, 'dp', 'tensor')
- out_grad: float32 [1024, 1024], P('tensor', 'dp')
- inner_grad: float32 [2, 1024, 2816], P(None, 'dp', 'tensor')
- outer_grad: float32 [2816, 1024], P('tensor', 'dp')
- tables_grad: float32 [3, 32, 16], P(None, 'dp', 'tensor')
Inputs may be any that keep to these rules, and one draw needn't show every extreme that they name: `page_counts`: true token count of each page; a page's tokens at or past it are padding that no query attends to. Some page is full and some page has the least count in every draw.
All inputs are finite; a program needn't handle non-finite values.
Results may differ from a plain program's by a relative error of at most 0.022.
Values may be sent and summed in bfloat16 or wider, within the bound.
A program may use at most 256 MiB of HBM per device.

v0:
```python
import math

import jax
import jax.numpy as jnp
import numpy as np
from jax import lax
from jax.sharding import PartitionSpec as P

HEAD_DIM = 64
BUCKETS = 32
REL_REACH = 128
CELLS = 64
PAGE_LEN = 1024


HIGHEST_PRECISION = lax.Precision.HIGHEST
TABLE_PRECISION = lax.Precision.HIGH
NORM_EPSILON = 1e-06
MASK_VALUE = -1e30


def bucket_table(offsets, bucket_total, max_reach):
    half_total = bucket_total // 2
    exact_limit = half_total // 2
    distance = np.abs(offsets).astype(np.int32)
    upper_side = (offsets > 0).astype(np.int32) * half_total
    safe_dist = np.maximum(distance, 1).astype(np.float32)
    ratio = np.log(safe_dist / np.float32(exact_limit)) / np.float32(
        math.log(max_reach / exact_limit)
    )
    far_bucket = exact_limit + np.floor(ratio * np.float32(half_total - exact_limit)).astype(
        np.int32
    )
    far_bucket = np.minimum(far_bucket, half_total - 1)
    return (upper_side + np.where(distance < exact_limit, distance, far_bucket)).astype(np.int32)


def offset_onehot(length):
    offsets = np.arange(2 * length - 1) - (length - 1)
    buckets = bucket_table(offsets, BUCKETS, REL_REACH)
    return jnp.asarray((buckets[:, None] == np.arange(BUCKETS)[None, :]).astype(np.float32))


def layout_onehot():
    cell_range = np.arange(CELLS)
    buckets = bucket_table(cell_range[None, :] - cell_range[:, None], BUCKETS, CELLS)
    return jnp.asarray(
        (buckets.reshape(-1)[:, None] == np.arange(BUCKETS)[None, :]).astype(np.float32)
    )


def gelu_tanh(values):
    return jax.nn.gelu(values, approximate=True)


def relative_bias(table_rows, length):
    values = jnp.dot(offset_onehot(length), table_rows, precision=HIGHEST_PRECISION).T
    heads_dev = values.shape[0]
    padded = jnp.pad(values, ((0, 0), (0, 1)))
    tiled = jnp.tile(padded, (1, length))
    skewed = tiled[:, : length * (2 * length - 1)].reshape(heads_dev, length, 2 * length - 1)
    return skewed[:, :, length - 1 :]


def relative_sums(dscore, length):
    heads_dev = dscore.shape[0]
    placed = jnp.pad(dscore, ((0, 0), (0, 0), (length - 1, 0)))
    flat = jnp.pad(placed.reshape(heads_dev, length * (2 * length - 1)), ((0, 0), (0, length)))
    return jnp.sum(flat.reshape(heads_dev, length, 2 * length), axis=1)[:, : 2 * length - 1]


def layout_values(tables):
    values = jnp.einsum("mn,snh->shm", layout_onehot(), tables[1:], precision=HIGHEST_PRECISION)
    return values.reshape(2, tables.shape[2], CELLS, CELLS)


def cell_onehots(page_cells):
    onehot = (page_cells[:, :, None] == jnp.arange(CELLS)[None, None, :]).astype(jnp.float32)
    length = page_cells.shape[1]
    joined = onehot.transpose(1, 0, 2).reshape(length, 2 * CELLS)
    return (onehot, joined)


def layout_bias(page_cells, lay_vals):
    onehot, joined = cell_onehots(page_cells)
    length = page_cells.shape[1]
    heads_dev = lay_vals.shape[1]
    rows_side = jnp.einsum("sia,shab->hisb", onehot, lay_vals, precision=TABLE_PRECISION)
    rows_side = rows_side.reshape(heads_dev, length, 2 * CELLS)
    return jnp.einsum("hic,jc->hij", rows_side, joined, precision=TABLE_PRECISION)


def layout_sums(dscore, page_cells):
    onehot, joined = cell_onehots(page_cells)
    length = page_cells.shape[1]
    heads_dev = dscore.shape[0]
    partial_rows = jnp.einsum("hij,jc->hic", dscore, joined, precision=TABLE_PRECISION)
    partial_rows = partial_rows.reshape(heads_dev, length, 2, CELLS)
    return jnp.einsum("sia,hisb->shab", onehot, partial_rows, precision=TABLE_PRECISION)


def page_scores(query, key_rows, count, page_cells, rel_bias, lay_vals):
    length = query.shape[0]
    scores = jnp.einsum("ihd,jhd->hij", query, key_rows, preferred_element_type=jnp.float32)
    scores = scores + rel_bias + layout_bias(page_cells, lay_vals)
    valid = jnp.arange(length) < count
    return jnp.where(valid[None, None, :], scores, MASK_VALUE)


def attend(projected, page_counts, layout_cells, rel_bias, lay_vals):
    total_rows = projected.shape[1]
    pages = page_counts.shape[0]
    length = total_rows // pages
    heads_dev = projected.shape[2] // HEAD_DIM
    split = projected.reshape(3, pages, length, heads_dev, HEAD_DIM)
    cells_pages = layout_cells.reshape(2, pages, length).transpose(1, 0, 2)

    def one_page(items):
        query, key_rows, value_rows, count, page_cells = items
        scores = page_scores(query, key_rows, count, page_cells, rel_bias, lay_vals)
        log_total = jax.nn.logsumexp(scores, axis=2)
        prob_low = jnp.exp(scores - log_total[:, :, None]).astype(jnp.bfloat16)
        context = jnp.einsum(
            "hij,jhd->ihd", prob_low, value_rows, preferred_element_type=jnp.float32
        )
        return (context.astype(jnp.bfloat16).reshape(length, heads_dev * HEAD_DIM), log_total)

    context, log_totals = lax.map(
        one_page, (split[0], split[1], split[2], page_counts, cells_pages)
    )
    return (context.reshape(total_rows, heads_dev * HEAD_DIM), log_totals)


def attend_back(projected, grad_context, log_totals, page_counts, layout_cells, rel_bias, lay_vals):
    total_rows = projected.shape[1]
    pages = page_counts.shape[0]
    length = total_rows // pages
    heads_dev = projected.shape[2] // HEAD_DIM
    split = projected.reshape(3, pages, length, heads_dev, HEAD_DIM)
    grad_split = grad_context.reshape(pages, length, heads_dev, HEAD_DIM)
    cells_pages = layout_cells.reshape(2, pages, length).transpose(1, 0, 2)

    def page_step(carry, items):
        rel_acc, lay_acc = carry
        query, key_rows, value_rows, grad_ctx, page_lse, count, page_cells = items
        scores = page_scores(query, key_rows, count, page_cells, rel_bias, lay_vals)
        prob = jnp.exp(scores - page_lse[:, :, None])
        grad_prob = jnp.einsum(
            "ihd,jhd->hij", grad_ctx, value_rows, preferred_element_type=jnp.float32
        )
        delta = jnp.sum(grad_prob * prob, axis=2, keepdims=True)
        dscore = prob * (grad_prob - delta)
        rel_acc = rel_acc + relative_sums(dscore, length)
        lay_acc = lay_acc + layout_sums(dscore, page_cells)
        score_low = dscore.astype(jnp.bfloat16)
        grad_query = jnp.einsum(
            "hij,jhd->ihd", score_low, key_rows, preferred_element_type=jnp.float32
        ).astype(jnp.bfloat16)
        grad_key = jnp.einsum(
            "hij,ihd->jhd", score_low, query, preferred_element_type=jnp.float32
        ).astype(jnp.bfloat16)
        grad_value = jnp.einsum(
            "hij,ihd->jhd", prob.astype(jnp.bfloat16), grad_ctx, preferred_element_type=jnp.float32
        ).astype(jnp.bfloat16)
        stacked = jnp.stack([grad_query, grad_key, grad_value]).reshape(
            3, length, heads_dev * HEAD_DIM
        )
        return ((rel_acc, lay_acc), stacked)

    init_sums = (
        jnp.zeros((heads_dev, 2 * length - 1), jnp.float32),
        jnp.zeros((2, heads_dev, CELLS, CELLS), jnp.float32),
    )
    (rel_acc, lay_acc), grads = lax.scan(
        page_step,
        init_sums,
        (split[0], split[1], split[2], grad_split, log_totals, page_counts, cells_pages),
    )
    grad_proj = grads.transpose(1, 0, 2, 3).reshape(3, total_rows, heads_dev * HEAD_DIM)
    rel_grad = jnp.dot(offset_onehot(length).T, rel_acc.T, precision=HIGHEST_PRECISION)
    lay_grad = jnp.einsum(
        "shm,mn->snh",
        lay_acc.reshape(2, heads_dev, CELLS * CELLS),
        layout_onehot(),
        precision=HIGHEST_PRECISION,
    )
    return (grad_proj, jnp.concatenate([rel_grad[None], lay_grad], axis=0))


def norm_back(rows, scale, gain, grad_normed):
    weighted = grad_normed * gain
    return scale * weighted - rows * scale**3 * jnp.mean(rows * weighted, axis=1, keepdims=True)


def forward_core(
    token_rows,
    norm_gains,
    attn_qkv,
    attn_out,
    ffn_in,
    page_counts,
    layout_cells,
    rel_bias,
    lay_vals,
):
    scale_one = lax.rsqrt(jnp.mean(token_rows * token_rows, axis=1, keepdims=True) + NORM_EPSILON)
    normed_one = (token_rows * scale_one * norm_gains[0]).astype(jnp.bfloat16)
    gathered_one = lax.all_gather(normed_one, "tensor", axis=0, tiled=True)
    projected = jnp.einsum(
        "td,cdk->ctk", gathered_one, attn_qkv, preferred_element_type=jnp.float32
    ).astype(jnp.bfloat16)
    context, log_totals = attend(projected, page_counts, layout_cells, rel_bias, lay_vals)
    attn_total = lax.psum_scatter(
        jnp.dot(context, attn_out, preferred_element_type=jnp.float32)
        .astype(jnp.bfloat16)
        .astype(jnp.float32)
        .astype(jnp.bfloat16),
        "tensor",
        scatter_dimension=0,
        tiled=True,
    ).astype(jnp.float32)
    resid = token_rows + attn_total
    scale_two = lax.rsqrt(jnp.mean(resid * resid, axis=1, keepdims=True) + NORM_EPSILON)
    normed_two = (resid * scale_two * norm_gains[1]).astype(jnp.bfloat16)
    gathered_two = lax.all_gather(normed_two, "tensor", axis=0, tiled=True)
    gate_up = jnp.einsum("td,cdf->ctf", gathered_two, ffn_in, preferred_element_type=jnp.float32)
    hidden = (gelu_tanh(gate_up[0]) * gate_up[1]).astype(jnp.bfloat16)
    return (
        scale_one,
        gathered_one,
        projected,
        context,
        log_totals,
        resid,
        scale_two,
        gathered_two,
        gate_up,
        hidden,
    )


def body(
    tokens,
    norm_gains,
    attn_qkv,
    attn_out,
    ffn_in,
    ffn_out,
    position_tables,
    page_counts,
    layout_cells,
    cotangent,
):
    token_rows = tokens.astype(jnp.float32)
    rel_bias = relative_bias(position_tables[0], PAGE_LEN)
    lay_vals = layout_values(position_tables)
    first = forward_core(
        token_rows,
        norm_gains,
        attn_qkv,
        attn_out,
        ffn_in,
        page_counts,
        layout_cells,
        rel_bias,
        lay_vals,
    )
    first_hidden = first[9]
    rows_part = first_hidden
    ffn_total = lax.psum_scatter(
        jnp.dot(rows_part, ffn_out, preferred_element_type=jnp.float32)
        .astype(jnp.bfloat16)
        .astype(jnp.float32)
        .astype(jnp.bfloat16),
        "tensor",
        scatter_dimension=0,
        tiled=True,
    ).astype(jnp.float32)
    layer_out = (first[5] + ffn_total).astype(jnp.bfloat16)
    cot_rows = lax.all_gather(cotangent, "tensor", axis=0, tiled=True)
    again_rows, cot_rows = lax.optimization_barrier((token_rows, cot_rows))
    saved = forward_core(
        again_rows,
        norm_gains,
        attn_qkv,
        attn_out,
        ffn_in,
        page_counts,
        layout_cells,
        rel_bias,
        lay_vals,
    )
    (
        scale_one,
        gathered_one,
        projected,
        context,
        log_totals,
        resid,
        scale_two,
        gathered_two,
        gate_up,
        hidden,
    ) = saved
    grad_hidden = jnp.einsum("td,fd->tf", cot_rows, ffn_out, preferred_element_type=jnp.float32)
    outer_grad = jnp.einsum("tf,td->fd", hidden, cot_rows, preferred_element_type=jnp.float32)
    gelu_value, gelu_back = jax.vjp(gelu_tanh, gate_up[0])
    grad_gate = gelu_back(grad_hidden * gate_up[1])[0].astype(jnp.bfloat16)
    grad_up = (grad_hidden * gelu_value).astype(jnp.bfloat16)
    grad_gate_up = jnp.stack([grad_gate, grad_up])
    inner_grad = jnp.einsum(
        "td,ctf->cdf", gathered_two, grad_gate_up, preferred_element_type=jnp.float32
    )
    rows_part = grad_gate_up
    grad_normed_two = lax.psum_scatter(
        jnp.einsum("ctf,cdf->td", rows_part, ffn_in, preferred_element_type=jnp.float32)
        .astype(jnp.bfloat16)
        .astype(jnp.float32)
        .astype(jnp.bfloat16),
        "tensor",
        scatter_dimension=0,
        tiled=True,
    ).astype(jnp.float32)
    grad_resid = cotangent.astype(jnp.float32) + norm_back(
        resid, scale_two, norm_gains[1], grad_normed_two
    )
    gain_two = jnp.sum(grad_normed_two * resid * scale_two, axis=0)
    resid_rows = lax.all_gather(grad_resid.astype(jnp.bfloat16), "tensor", axis=0, tiled=True)
    out_grad = jnp.einsum("tk,td->kd", context, resid_rows, preferred_element_type=jnp.float32)
    grad_context = jnp.einsum(
        "td,kd->tk", resid_rows, attn_out, preferred_element_type=jnp.float32
    ).astype(jnp.bfloat16)
    grad_proj, tables_grad = attend_back(
        projected, grad_context, log_totals, page_counts, layout_cells, rel_bias, lay_vals
    )
    qkv_grad = jnp.einsum(
        "td,ctk->cdk", gathered_one, grad_proj, preferred_element_type=jnp.float32
    )
    rows_part = grad_proj
    grad_normed_one = lax.psum_scatter(
        jnp.einsum("ctk,cdk->td", rows_part, attn_qkv, preferred_element_type=jnp.float32)
        .astype(jnp.bfloat16)
        .astype(jnp.float32)
        .astype(jnp.bfloat16),
        "tensor",
        scatter_dimension=0,
        tiled=True,
    ).astype(jnp.float32)
    tokens_grad = grad_resid + norm_back(token_rows, scale_one, norm_gains[0], grad_normed_one)
    gain_one = jnp.sum(grad_normed_one * token_rows * scale_one, axis=0)
    gains_grad = lax.psum_scatter(
        jnp.stack([gain_one, gain_two]), ("dp", "tensor"), scatter_dimension=1, tiled=True
    )
    qkv_summed, inner_summed, out_summed, outer_summed, tables_summed = (
        lax.psum_scatter(
            qkv_grad.astype(jnp.bfloat16), "dp", scatter_dimension=1, tiled=True
        ).astype(jnp.float32),
        lax.psum_scatter(
            inner_grad.astype(jnp.bfloat16), "dp", scatter_dimension=1, tiled=True
        ).astype(jnp.float32),
        lax.psum_scatter(
            out_grad.astype(jnp.bfloat16), "dp", scatter_dimension=1, tiled=True
        ).astype(jnp.float32),
        lax.psum_scatter(
            outer_grad.astype(jnp.bfloat16), "dp", scatter_dimension=1, tiled=True
        ).astype(jnp.float32),
        lax.psum_scatter(
            tables_grad.astype(jnp.bfloat16), "dp", scatter_dimension=1, tiled=True
        ).astype(jnp.float32),
    )
    return (
        layer_out,
        tokens_grad,
        gains_grad,
        qkv_summed,
        out_summed,
        inner_summed,
        outer_summed,
        tables_summed,
    )


def solution(mesh):
    return jax.shard_map(
        body,
        mesh=mesh,
        in_specs=(
            P(("dp", "tensor"), None),
            P(),
            P(None, None, "tensor"),
            P("tensor", None),
            P(None, None, "tensor"),
            P("tensor", None),
            P(None, None, "tensor"),
            P("dp"),
            P(None, "dp"),
            P(("dp", "tensor"), None),
        ),
        out_specs=(
            P(("dp", "tensor"), None),
            P(("dp", "tensor"), None),
            P(None, ("dp", "tensor")),
            P(None, "dp", "tensor"),
            P("tensor", "dp"),
            P(None, "dp", "tensor"),
            P("tensor", "dp"),
            P(None, "dp", "tensor"),
        ),
        check_vma=False,
    )
```

profile of v0, /device:TPU:0, one launch (start us, length us, event | category | flops | bytes accessed | tf_op | source)
XLA Modules:
  0.0 2264.0 jit_solution(10170065226509743736)
XLA Ops:
  11.5 81.6 %all-gather.11.cloned.1.call-done = bf16[2048,1024]{1,0:T(8,128)(2,1)} async-done(((bf16[512,1024]{1,0:T(8,128)(2,1)}), bf16[2048,1024]{1,0:T(8,128)(2,1)}) %all-gather.11.cloned.1.call-update) | async-done | bytes 4194320 | tf_op jit(solution)/shard_map/all_gather | solution.py:280
  113.7 38.0 %copy.157 = f32[1,4,1024,2048]{3,1,2,0:T(4,128)} copy(f32[1,4,1024,2048]{3,2,1,0:T(8,128)} %broadcast_bitcast_fusion) | data formatting | bytes 67108864
  151.7 23.8 %slice.90 = f32[4,2096128]{1,0:T(4,128)} slice(f32[4,2097152]{1,0:T(4,128)} %bitcast.428), slice={[0:4], [0:2096128]} | slice | bytes 67076096 | tf_op jit(solution)/shard_map/slice | solution.py:61
  175.5 94.2 %reshape.284 = f32[8384512]{0:T(1024)} reshape(f32[4,2096128]{1,0:T(4,128)} %slice.90) | data formatting | bytes 67076096
  269.7 49.8 %reshape.234 = f32[4,1024,2047]{2,1,0:T(8,128)} reshape(f32[8384512]{0:T(1024)} %reshape.284) | data formatting | bytes 67076096 | tf_op jit(solution)/shard_map/reshape | solution.py:61
  383.8 108.1 %while.40 = (s32[]{:T(128)}, bf16[2,1024,256]{2,1,0:T(8,128)(2,1)}, f32[2,4,1024]{2,1,0:T(4,128)}, bf16[2,1024,4,64]{1,3,2,0:T(8,128)(2,1)}, s32[2]{0:T(128)}, /...) while((s32[]{:T(128)}, bf16[2,1024,256]{2,1,0:T(8,128)(2,1)}, ...), condition=%wide.region_12.13_spmd, body=%wide.region_9.12_spmd.sunk | while | flops 4530406400 | bytes 113618096 | solution.py:128
  396.8 19.2 fusion.281
  497.0 75.1 %reduce-scatter.26.cloned.1.call-done = bf16[512,1024]{1,0:T(8,128)(2,1)} async-done(((bf16[2048,1024]{1,0:T(8,128)(2,1)}), bf16[512,1024]{1,0:T(8,128)(2,1)}) %reduce-scatter.26.cloned.1.call-update) | async-done | bytes 1048592 | tf_op jit(solution)/shard_map/reduce_scatter | solution.py:213
  577.3 81.4 %all-gather.15.cloned.1.call-done = bf16[2048,1024]{1,0:T(8,128)(2,1)} async-done(((bf16[512,1024]{1,0:T(8,128)(2,1)}), bf16[2048,1024]{1,0:T(8,128)(2,1)}) %all-gather.15.cloned.1.call-update) | async-done | bytes 4194320 | tf_op jit(solution)/shard_map/all_gather | solution.py:225
  685.4 75.4 %reduce-scatter.28.cloned.1.call-done = bf16[512,1024]{1,0:T(8,128)(2,1)} async-done(((bf16[2048,1024]{1,0:T(8,128)(2,1)}), bf16[512,1024]{1,0:T(8,128)(2,1)}) %reduce-scatter.28.cloned.1.call-update) | async-done | bytes 1048592 | tf_op jit(solution)/shard_map/reduce_scatter | solution.py:315
  768.8 80.9 %all-gather.17.cloned.1.call-done = bf16[2048,1024]{1,0:T(8,128)(2,1)} async-done(((bf16[512,1024]{1,0:T(8,128)(2,1)}), bf16[2048,1024]{1,0:T(8,128)(2,1)}) %all-gather.17.cloned.1.call-update) | async-done | bytes 4194320 | tf_op jit(solution)/shard_map/all_gather | solution.py:328
  862.8 531.5 %while.41 = (s32[]{:T(128)}, f32[4,2047]{1,0:T(4,128)}, f32[2,4,64,64]{2,3,1,0:T(8,128)S(1)}, bf16[2,3,1024,256]{3,2,0,1:T(8,128)(2,1)}, s32[2]{0:T(128)}, /*ind...) while((s32[]{:T(128)}, f32[4,2047]{1,0:T(4,128)}, ...), condition=%wide.region_20.21_spmd.clone, body=%wide.region_17.20_spmd.clone.sunk | while | flops 9586938880 | bytes 645969984 | solution.py:174
  877.3 19.6 fusion.303
  976.0 19.9 pad.19.clone.2
  995.9 46.4 %reshape.288 = f32[8384512]{0:T(1024)} reshape(f32[4,1024,2047]{2,1,0:T(8,128)} %pad.19.clone.2) | data formatting | bytes 67076096 | tf_op jit(solution)/shard_map/while
  1042.4 40.4 %reshape.289 = f32[4,2096128]{1,0:T(4,128)} reshape(f32[8384512]{0:T(1024)} %reshape.288) | data formatting | bytes 67076096 | tf_op jit(solution)/shard_map/while/body/eval_jaxpr/reshape | solution.py:68
  1082.8 22.9 %pad.54 = f32[4,2097152]{1,0:T(4,128)} pad(f32[4,2096128]{1,0:T(4,128)} %reshape.289, f32[]{:T(128)} %constant.105.clone.1..sunk), padding=0_0x0_1024 | pad | bytes 67092484 | tf_op jit(solution)/shard_map/while/body/eval_jaxpr/jit(_pad)/pad | solution.py:68
  1139.8 19.6 fusion.303
  1238.8 19.9 pad.19.clone.2
  1258.6 46.2 %reshape.288 = f32[8384512]{0:T(1024)} reshape(f32[4,1024,2047]{2,1,0:T(8,128)} %pad.19.clone.2) | data formatting | bytes 67076096 | tf_op jit(solution)/shard_map/while
  1304.8 40.4 %reshape.289 = f32[4,2096128]{1,0:T(4,128)} reshape(f32[8384512]{0:T(1024)} %reshape.288) | data formatting | bytes 67076096 | tf_op jit(solution)/shard_map/while/body/eval_jaxpr/reshape | solution.py:68
  1345.3 22.9 %pad.54 = f32[4,2097152]{1,0:T(4,128)} pad(f32[4,2096128]{1,0:T(4,128)} %reshape.289, f32[]{:T(128)} %constant.105.clone.1..sunk), padding=0_0x0_1024 | pad | bytes 67092484 | tf_op jit(solution)/shard_map/while/body/eval_jaxpr/jit(_pad)/pad | solution.py:68
  1402.4 75.4 %reduce-scatter.30.cloned.1.call-done = bf16[512,1024]{1,0:T(8,128)(2,1)} async-done(((bf16[2048,1024]{1,0:T(8,128)(2,1)}), bf16[512,1024]{1,0:T(8,128)(2,1)}) %reduce-scatter.30.cloned.1.call-update) | async-done | bytes 1048592 | tf_op jit(solution)/shard_map/reduce_scatter | solution.py:340
  1485.7 81.4 %all-gather.7.cloned.1.call-done = bf16[2048,1024]{1,0:T(8,128)(2,1)} async-done(((bf16[512,1024]{1,0:T(8,128)(2,1)}), bf16[2048,1024]{1,0:T(8,128)(2,1)}) %all-gather.7.cloned.1.call-update) | async-done | bytes 4194320 | tf_op jit(solution)/shard_map/all_gather | solution.py:208
  1601.7 106.5 %while.39 = (s32[]{:T(128)}, bf16[2,1024,256]{2,1,0:T(8,128)(2,1)}, bf16[2,1024,4,64]{1,3,2,0:T(8,128)(2,1)}, s32[2]{0:T(128)}, bf16[2,1024,4,64]{1,3,2,0:T(8,12...) while((s32[]{:T(128)}, bf16[2,1024,256]{2,1,0:T(8,128)(2,1)}, ...), condition=%wide.region_4.5_spmd, body=%wide.region_1.4_spmd.sunk | while | flops 4530390016 | bytes 113568936 | solution.py:128
  1713.4 75.0 %reduce-scatter.22.cloned.1.call-done = bf16[512,1024]{1,0:T(8,128)(2,1)} async-done(((bf16[2048,1024]{1,0:T(8,128)(2,1)}), bf16[512,1024]{1,0:T(8,128)(2,1)}) %reduce-scatter.22.cloned.1.call-update) | async-done | bytes 1048592 | tf_op jit(solution)/shard_map/reduce_scatter | solution.py:213
  1854.8 19.8 all-gather.9.cloned.1.call-done
  1890.3 24.7 %reduce-scatter.40.cloned.1.call-done = bf16[128,704]{1,0:T(8,128)(2,1)} async-done(((bf16[1024,704]{1,0:T(8,128)(2,1)}), bf16[128,704]{1,0:T(8,128)(2,1)}) %reduce-scatter.40.cloned.1.call-update) | async-done | bytes 180240
  1916.8 46.3 %reduce-scatter.38.cloned.1.call-done = bf16[128,1408]{1,0:T(8,128)(2,1)} async-done(((bf16[1024,1408]{1,0:T(8,128)(2,1)}), bf16[128,1408]{1,0:T(8,128)(2,1)}) %reduce-scatter.38.cloned.1.call-update) | async-done | bytes 360464
  2002.3 40.0 %reduce-scatter.34.cloned.1.call-done = bf16[128,768]{1,0:T(8,128)(2,1)} async-done(((bf16[1024,768]{1,0:T(8,128)(2,1)}), bf16[128,768]{1,0:T(8,128)(2,1)}) %reduce-scatter.34.cloned.1.call-update) | async-done | bytes 196624
  2044.4 134.1 %reduce-scatter.32.cloned.1.call-done = f32[32,2]{1,0:T(8,128)} async-done(((f32[1024,2]{1,0:T(8,128)}), f32[32,2]{1,0:T(8,128)}) %reduce-scatter.32.cloned.1.call-update) | async-done | bytes 272
  2179.8 74.0 %reduce-scatter.24.cloned.1.call-done = bf16[512,1024]{1,0:T(8,128)(2,1)} async-done(((bf16[2048,1024]{1,0:T(8,128)(2,1)}), bf16[512,1024]{1,0:T(8,128)(2,1)}) %reduce-scatter.24.cloned.1.call-update) | async-done | bytes 1048592 | tf_op jit(solution)/shard_map/reduce_scatter | solution.py:270
  (314 shorter events, 752.8 us)
Async XLA Ops:
  7.2 651.5 %copy-start = (bf16[2,1024,704]{1,2,0:T(8,128)(2,1)S(1)}, bf16[2,1024,704]{1,2,0:T(8,128)(2,1)}, u32[]{:S(2)}) copy-start(bf16[2,1024,704]{1,2,0:T(8,128)(2,1)} %param.24) | copy-start | bytes 8650756
  7.2 85.9 %all-gather.11.cloned.1.call-start = ((), (), s32[]{:S(2)}) async-start(), calls=%async_computation.14 | async-start | bytes 5242880 | tf_op jit(solution)/shard_map/all_gather | solution.py:280
  7.9 91.1 %copy-start.16 = (f32[4096,32,1]{0,1,2:T(8,128)S(1)}, f32[4096,32,1]{0,1,2:T(8,128)}, u32[]{:S(2)}) copy-start(f32[4096,32,1]{0,1,2:T(8,128)} %constant.127) | copy-start | bytes 1572868
  7.9 91.1 %copy-start.29 = (f32[3,32,4]{1,2,0:T(4,128)S(1)}, f32[3,32,4]{1,2,0:T(4,128)}, u32[]{:S(2)}) copy-start(f32[3,32,4]{1,2,0:T(4,128)} %param.26) | copy-start | bytes 4612
  7.9 341.4 %all-gather.13.cloned.1.call-start = ((), (), s32[]{:S(2)}) async-start(), calls=%async_computation.15 | async-start | bytes 5242880 | tf_op jit(solution)/shard_map/all_gather | solution.py:208
  11.5 87.5 %copy-start.21 = (f32[1,1024]{1,0:T(1,128)}, f32[1,1024]{1,0:T(1,128)S(1)}, u32[]{:S(2)}) copy-start(f32[1,1024]{1,0:T(1,128)S(1)} %get-tuple-element.537) | copy-start | bytes 12292
  98.9 473.2 %reduce-scatter.26.cloned.1.call-start = ((), (), s32[]{:S(2)}) async-start(), calls=%async_computation.16 | async-start | bytes 5242880 | tf_op jit(solution)/shard_map/reduce_scatter | solution.py:213
  496.7 77.8 %copy-start.19 = (f32[1,1024]{1,0:T(1,128)S(1)}, f32[1,1024]{1,0:T(1,128)}, u32[]{:S(2)}) copy-start(f32[1,1024]{1,0:T(1,128)} %get-tuple-element.536) | copy-start | bytes 12292
  496.7 162.0 %all-gather.15.cloned.1.call-start = ((), (), s32[]{:S(2)}) async-start(), calls=%async_computation.17 | async-start | bytes 5242880 | tf_op jit(solution)/shard_map/all_gather | solution.py:225
  577.3 183.6 %reduce-scatter.28.cloned.1.call-start = ((), (), s32[]{:S(2)}) async-start(), calls=%async_computation.18 | async-start | bytes 5242880 | tf_op jit(solution)/shard_map/reduce_scatter | solution.py:315
  685.4 164.3 %all-gather.17.cloned.1.call-start = ((), (), s32[]{:S(2)}) async-start(), calls=%async_computation.19 | async-start | bytes 5242880 | tf_op jit(solution)/shard_map/all_gather | solution.py:328
  768.3 709.5 %reduce-scatter.30.cloned.1.call-start = ((), (), s32[]{:S(2)}) async-start(), calls=%async_computation.20 | async-start | bytes 5242880 | tf_op jit(solution)/shard_map/reduce_scatter | solution.py:340
  863.0 14.4 copy-start.6
  1105.7 19.0 copy-start.17
  1105.7 19.6 copy-start.7
  1125.5 14.4 copy-start.6
  1368.2 19.0 copy-start.17
  1368.2 19.6 copy-start.7
  1402.3 75.5 %copy-start.22 = (f32[1,1024]{1,0:T(1,128)S(1)}, f32[1,1024]{1,0:T(1,128)}, u32[]{:S(2)}) copy-start(f32[1,1024]{1,0:T(1,128)} %copy-done.21) | copy-start | bytes 12292
  1402.3 75.5 %copy-start.24 = (f32[512]{0:T(512)S(1)}, f32[512]{0:T(512)}, u32[]{:S(2)}) copy-start(f32[512]{0:T(512)} %copy-done.23) | copy-start | bytes 6148
  1402.3 78.6 %copy-start.28 = (f32[512]{0:T(512)S(1)}, f32[512]{0:T(512)}, u32[]{:S(2)}) copy-start(f32[512]{0:T(512)} %get-tuple-element.538) | copy-start | bytes 6148
  1402.4 164.7 %all-gather.7.cloned.1.call-start = ((), (), s32[]{:S(2)}) async-start(), calls=%async_computation.10 | async-start | bytes 5242880 | tf_op jit(solution)/shard_map/all_gather | solution.py:208
  1485.6 302.7 %reduce-scatter.22.cloned.1.call-start = ((), (), s32[]{:S(2)}) async-start(), calls=%async_computation.11 | async-start | bytes 5242880 | tf_op jit(solution)/shard_map/reduce_scatter | solution.py:213
  1712.9 77.4 %copy-start.20 = (f32[1,1024]{1,0:T(1,128)S(1)}, f32[1,1024]{1,0:T(1,128)}, u32[]{:S(2)}) copy-start(f32[1,1024]{1,0:T(1,128)} %get-tuple-element.536) | copy-start | bytes 12292
  1712.9 161.7 %all-gather.9.cloned.1.call-start = ((), (), s32[]{:S(2)}) async-start(), calls=%async_computation.12 | async-start | bytes 5242880 | tf_op jit(solution)/shard_map/all_gather | solution.py:225
  1793.2 121.8 %reduce-scatter.40.cloned.1.call-start = ((), (), s32[]{:S(2)}) async-start(), calls=%async_computation.25 | async-start | bytes 1769472
  1806.4 156.7 %reduce-scatter.38.cloned.1.call-start = ((), (), s32[]{:S(2)}) async-start(), calls=%async_computation.24 | async-start | bytes 3244032
  1833.4 167.3 %reduce-scatter.36.cloned.1.call-start = ((), (), s32[]{:S(2)}) async-start(), calls=%async_computation.23 | async-start | bytes 589824
  1838.3 204.0 %reduce-scatter.34.cloned.1.call-start = ((), (), s32[]{:S(2)}) async-start(), calls=%async_computation.22 | async-start | bytes 1769472
  1853.6 324.9 %reduce-scatter.32.cloned.1.call-start = ((), (), s32[]{:S(2)}) async-start(), calls=%async_computation.21 | async-start | bytes 540672
  1854.8 399.1 %reduce-scatter.24.cloned.1.call-start = ((), (), s32[]{:S(2)}) async-start(), calls=%async_computation.13 | async-start | bytes 5242880 | tf_op jit(solution)/shard_map/reduce_scatter | solution.py:270
  1888.4 79.1 %copy-start.14 = (f32[2,4,64,64]{2,3,1,0:T(8,128)S(1)}, f32[2,4,64,64]{2,3,1,0:T(8,128)}, u32[]{:S(2)}) copy-start(f32[2,4,64,64]{2,3,1,0:T(8,128)} %copy-done.13) | copy-start | bytes 393220
  (32 other events, 193.4 us)
Sparse Core Ops, SparseCore 0:
  9.6 83.4 all-gather.10
  99.0 79.2 all-gather.12
  496.8 75.2 reduce-scatter.25
  577.4 81.2 all-gather.14
  685.5 75.2 reduce-scatter.27
  768.4 81.2 all-gather.16
  1402.5 75.2 reduce-scatter.29
  1485.7 81.2 all-gather.6
  1713.0 75.2 reduce-scatter.21
  1793.4 81.2 all-gather.8
  1878.0 36.9 reduce-scatter.39
  1918.2 44.8 reduce-scatter.37
  1966.5 34.1 reduce-scatter.35
  2003.8 38.4 reduce-scatter.33
  2044.4 134.0 reduce-scatter.31
  2180.7 73.0 reduce-scatter.23
where the time goes:
time: 2270 us; the launch traced here: 2260 us
  waiting for transfers between devices  982 us (43%)
  local copies, waits for them, and re-layouts  699 us (31%)
  matrix products  404 us (18%)
  other arithmetic  142 us (6%)
    unnamed x21, waiting for transfers between devices  262 us
    unnamed x73, local copies, waits for them, and re-layouts  189 us
    reduce_scatter x2, waiting for transfers between devices, forward_core(): lax.psum_scatter(jnp.dot(context, attn_out, preferred_element_type=jnp.fl...  150 us
    while x48, local copies, waits for them, and re-layouts  135 us
    dot_general x6, matrix products, page_scores(): jnp.einsum('ihd,jhd->hij', query, key_rows, preferred_element_type=jnp.fl...  116 us
    all_gather x2, waiting for transfers between devices, forward_core(): gathered_two = lax.all_gather(normed_two, 'tensor', axis=0, tiled=True)  101 us
    all_gather x1, waiting for transfers between devices, body(): cot_rows = lax.all_gather(cotangent, 'tensor', axis=0, tiled=True)  81.6 us
    all_gather x2, waiting for transfers between devices, forward_core(): gathered_one = lax.all_gather(normed_one, 'tensor', axis=0, tiled=True)  81.4 us
  transfers between devices with their start and end apart: 16, of which 15 were waited for; matrix products, arithmetic and copies ran while one was open for 15% of the time, Pallas kernels for 0%

commit v1 on v0

--- a/solution.py
+++ b/solution.py
@@ -4,6 +4,8 @@
 import jax.numpy as jnp
 import numpy as np
 from jax import lax
+from jax.experimental import pallas as pl
+from jax.experimental.pallas import tpu as pltpu
 from jax.sharding import PartitionSpec as P
 
 HEAD_DIM = 64
@@ -239,7 +241,7 @@
     )
 
 
-def body(
+def general_body(
     tokens,
     norm_gains,
     attn_qkv,
@@ -380,9 +382,1136 @@
     )
 
 
+PLANES = 4
+RING = 4
+CORES = 2
+BLOCK = 256
+HALF = 128
+ATT = 512
+UNITS = 384
+FFW = 3 * UNITS
+VMEM_BYTES = 60 * 1024 * 1024
+F32 = jnp.float32
+BF16 = jnp.bfloat16
+NT = (((1,), (1,)), ((), ()))
+TN = (((0,), (0,)), ((), ()))
+NN = (((1,), (0,)), ((), ()))
+
+
+def page_plan(mesh):
+    return mesh.shape["dp"] == PLANES * CORES and mesh.shape["tensor"] == RING
+
+
+def dot(left, right, dims=NN):
+    return lax.dot_general(left, right, dims, preferred_element_type=F32)
+
+
+def shaped(shape, dtype=BF16):
+    return jax.ShapeDtypeStruct(shape, dtype)
+
+
+def columns(plane, r):
+    return pl.ds(pl.multiple_of((plane ^ r) * BLOCK, BLOCK), BLOCK)
+
+
+def pair_lane(rows):
+    return lax.broadcasted_iota(jnp.int32, (rows, 2 * HEAD_DIM), 1)
+
+
+MESH = pl.DeviceIdType.MESH
+
+
+def here():
+    group, ring = lax.axis_index("dp"), lax.axis_index("tensor")
+    return group // CORES, group % CORES, ring
+
+
+def device(plane, core, ring):
+    return (plane * CORES + core, ring)
+
+
+def greet(partners):
+    barrier = pltpu.get_barrier_semaphore()
+    for partner in partners:
+        pl.semaphore_signal(barrier, inc=1, device_id=partner, device_id_type=MESH)
+    pl.semaphore_wait(barrier, len(partners))
+
+
+class Lines:
+    def __init__(self, send_sems, recv_sems):
+        self.send_sems, self.recv_sems, self.open = send_sems, recv_sems, {}
+
+    def make(self, name, source, target, partner):
+        at = len(self.open)
+        self.open[name] = pltpu.make_async_remote_copy(
+            src_ref=source,
+            dst_ref=target,
+            send_sem=self.send_sems.at[at],
+            recv_sem=self.recv_sems.at[at],
+            device_id=partner,
+            device_id_type=MESH,
+        )
+        return self.open[name]
+
+    def start(self, name, source, target, partner):
+        self.make(name, source, target, partner).start()
+
+    def arrived(self, *names):
+        for name in names:
+            self.open[name].wait_recv()
+
+    def sent(self, *names):
+        for name in names or list(self.open):
+            self.open[name].wait_send()
+
+
+class Gather:
+    def __init__(self, lines, tag, own, full, where):
+        self.lines, self.tag, self.own, self.full = lines, tag, own, full
+        self.plane, self.core, self.ring = where
+
+    def ring_start(self, k):
+        self.lines.start(
+            (self.tag, "z", k),
+            self.own.at[0:BLOCK],
+            self.full.at[k, 0:BLOCK],
+            device(self.plane, self.core, (self.ring + RING - k) % RING),
+        )
+
+    def plane_start(self, k):
+        self.lines.arrived((self.tag, "z", k))
+        for name, r in (("x", 1), ("y", 2)):
+            self.lines.start(
+                (self.tag, name, k),
+                self.full.at[k, 0:BLOCK],
+                self.full.at[k, r * BLOCK : (r + 1) * BLOCK],
+                device(self.plane ^ r, self.core, self.ring),
+            )
+
+    def corner_start(self, k):
+        for name, r, half, goal in (("x", 1, 0, 2), ("y", 2, 1, 1)):
+            self.lines.arrived((self.tag, name, k))
+            self.lines.start(
+                (self.tag, "corner" + name, k),
+                self.full.at[k, r * BLOCK + half * HALF : r * BLOCK + (half + 1) * HALF],
+                self.full.at[k, 3 * BLOCK + half * HALF : 3 * BLOCK + (half + 1) * HALF],
+                device(self.plane ^ goal, self.core, self.ring),
+            )
+
+    def finish(self, k):
+        self.lines.arrived((self.tag, "cornerx", k), (self.tag, "cornery", k))
+
+
+def own_attention(core, plane, qkv, out, target):
+    for r in range(PLANES):
+        rows, place = columns(plane, r), slice(r * BLOCK, (r + 1) * BLOCK)
+        mine = pl.ds(pl.multiple_of(core * HALF, HALF), HALF)
+        target[place, 0:HALF] = out[mine, rows].astype(F32).T.astype(BF16)
+        for m in range(3):
+            target[place, (m + 1) * HALF : (m + 2) * HALF] = qkv[m, rows, mine]
+
+
+def own_ffn(core, plane, inner, outer, target):
+    units = inner.shape[2]
+    for which, first, count in ((0, 0, UNITS), (1, UNITS, units - UNITS)):
+
+        @pl.when(core == which)
+        def _():
+            for r in range(PLANES):
+                rows, place = columns(plane, r), slice(r * BLOCK, (r + 1) * BLOCK)
+                parts = [outer[first : first + count, rows].astype(F32).T.astype(BF16)]
+                parts += [inner[m, rows, first : first + count] for m in range(2)]
+                for m, part in enumerate(parts):
+                    target[place, m * UNITS : m * UNITS + count] = part
+                    if count < UNITS:
+                        target[place, m * UNITS + count : (m + 1) * UNITS] = jnp.zeros(
+                            (BLOCK, UNITS - count), BF16
+                        )
+
+
+def place_rows(plane, core, near, far, full):
+    rows = near.shape[0]
+    for source, half in ((near, core), (far, 1 - core)):
+        for r in range(PLANES):
+            full[pl.ds(pl.multiple_of(half * rows, rows), rows), r * BLOCK : (r + 1) * BLOCK] = (
+                source[:, columns(plane, r)]
+            )
+
+
+def split_bf16(values):
+    parts = []
+    for _ in range(3):
+        part = values.astype(BF16)
+        parts.append(part)
+        values = values - part.astype(F32)
+    return parts
+
+
+def bias_pieces(tables, near_hot, cell_hot, layout, near):
+    parts = split_bf16(tables)
+    rel = sum(dot(part, near_hot[...]) for part in parts)
+    cells = dot(parts[0], cell_hot[...])
+    heads = tables.shape[0] // 3
+    for h in range(heads):
+        near[h] = rel[h : h + 1, :]
+        toeplitz = []
+        for axis in range(2):
+            row = jnp.broadcast_to(cells[(axis + 1) * heads + h : (axis + 1) * heads + h + 1], (CELLS, HALF))
+            toeplitz.append(pltpu.roll(row, CELLS, 1, stride=1, stride_axis=0))
+        side = lax.broadcasted_iota(jnp.int32, (CELLS, HALF), 1)
+        first = toeplitz[0]
+        layout[h, 0:CELLS, 0:HALF] = jnp.where(
+            side < CELLS, first, pltpu.roll(first, CELLS, 1)
+        ).astype(BF16)
+        layout[h, 0:CELLS, HALF:] = jnp.zeros((CELLS, HALF), BF16)
+        layout[h, CELLS:, 0:HALF] = jnp.zeros((CELLS, HALF), BF16)
+        layout[h, CELLS:, HALF:] = jnp.where(side < CELLS, toeplitz[1], 0.0).astype(BF16)
+
+
+def forward_kernel(
+    tokens, cot, gains, qkv_w, out_w, ffn_in, ffn_out, tables, ints, near_hot, cell_hot,
+    att_full, ffn_full, prob_full, full, gains_here, normed_t, resid, normed_two, normed_two_t,
+    cot_full, cot_t, qkv, context, inverse, cells_t, cells_twice, cell_tail,
+    near_x, far_x, near_g, far_g, other_ints, table_parts, table_rows, layout, near,
+    own_ffn_w, ffn_in_v, ffn_out_v, normed, weights, cells, queries, keys, scores, prob,
+    mixed_all, out_rows, mine_out, other_out,
+    send_sems, recv_sems, local_sems,
+):
+    plane, core, ring = where = here()
+    native = core == ring % 2
+    rows = tokens.shape[0]
+    length = 2 * rows
+    partner = device(plane, 1 - core, ring)
+    swap = device(plane, 1 - core, ring ^ 1)
+    ring_others = [device(plane, core, (ring + RING - k) % RING) for k in range(1, RING)]
+    neighbours = [device(plane ^ 1, core, ring), device(plane ^ 2, core, ring)]
+    lines = Lines(send_sems, recv_sems)
+    load_in = pltpu.make_async_copy(ffn_in, ffn_in_v, local_sems.at[0])
+    load_out = pltpu.make_async_copy(ffn_out, ffn_out_v, local_sems.at[1])
+    load_in.start()
+    load_out.start()
+    greet([partner, swap] + ring_others + neighbours)
+
+    def swap_rows(tag, source, near_rows, far_rows):
+        lines.make((tag, "swap"), source, near_rows, swap)
+        lines.make((tag, "give"), source, far_rows, partner)
+        lines.make((tag, "pass"), near_rows, far_rows, partner)
+
+        @pl.when(native)
+        def _():
+            lines.open[tag, "give"].start()
+            keep = pltpu.make_async_copy(source, near_rows, local_sems.at[2])
+            keep.start()
+            keep.wait()
+
+        @pl.when(jnp.logical_not(native))
+        def _():
+            lines.open[tag, "swap"].start()
+
+    def swap_pass(tag):
+        @pl.when(jnp.logical_not(native))
+        def _():
+            lines.arrived((tag, "swap"))
+            lines.open[tag, "pass"].start()
+            lines.arrived((tag, "give"))
+
+        @pl.when(native)
+        def _():
+            lines.arrived((tag, "pass"))
+
+    def swap_sent(tag):
+        @pl.when(jnp.logical_not(native))
+        def _():
+            lines.sent((tag, "swap"), (tag, "pass"))
+
+        @pl.when(native)
+        def _():
+            lines.sent((tag, "give"))
+
+    swap_rows("x", tokens, near_x, far_x)
+    lines.start("ints", ints, other_ints, partner)
+    table_parts[0] = tables[...]
+    for k in range(1, RING):
+        lines.start(("tables", k), tables, table_parts.at[k], ring_others[k - 1])
+    own_attention(core, plane, qkv_w, out_w, weights)
+    keep_weights = pltpu.make_async_copy(weights, att_full.at[0], local_sems.at[3])
+    keep_weights.start()
+    att = Gather(lines, "att", weights, att_full, where)
+    ffn = Gather(lines, "ffn", own_ffn_w, ffn_full, where)
+    keep_weights.wait()
+    att.own = att_full.at[0]
+    for k in range(1, RING):
+        att.ring_start(k)
+
+    lines.arrived("ints")
+    page = ring // 2
+    picked = []
+    for first in (0, 2, 4):
+        own_row = ints[pl.ds(first + page, 1), :]
+        other_row = other_ints[pl.ds(first + page, 1), :]
+        picked.append(jnp.where(native, own_row, other_row))
+    spot = lax.broadcasted_iota(jnp.int32, (CELLS, length), 0)
+    cells_x = (jnp.broadcast_to(picked[0], (CELLS, length)) == spot).astype(F32)
+    cells_y = (jnp.broadcast_to(picked[1], (CELLS, length)) == spot).astype(F32)
+    position = lax.broadcasted_iota(jnp.int32, (CELLS, length), 1)
+    tail = jnp.where((spot < 16) & (spot % 8 == position // HALF), 1.0, 0.0)
+    hidden_key = (spot == 16) & (position >= jnp.broadcast_to(picked[2], (CELLS, length)))
+    tail = jnp.where(hidden_key, MASK_VALUE, tail)
+    flipped = CELLS - 1 - spot
+    for axis in range(2):
+        turned = (jnp.broadcast_to(picked[axis], (CELLS, length)) == flipped).astype(F32)
+        cells_t[axis * CELLS : (axis + 1) * CELLS, :] = turned.astype(BF16)
+    cells[...] = jnp.concatenate([cells_x, cells_y], axis=0).T.astype(BF16)
+    cells_twice[...] = jnp.concatenate([cells_x, cells_x], axis=0).T.astype(BF16)
+    cell_tail[...] = jnp.concatenate([cells_y, tail], axis=0).T.astype(BF16)
+    for k in range(1, RING):
+        lines.arrived(("tables", k))
+    for k in range(RING):
+        for axis in range(3):
+            first = axis * 2 * RING + 2 * k
+            table_rows[first : first + 2, :] = table_parts[k, pl.ds(4 * axis + 2 * core, 2), :]
+    bias_pieces(table_rows[...], near_hot, cell_hot, layout, near)
+
+    for r in range(PLANES):
+        gains_here[:, r * BLOCK : (r + 1) * BLOCK] = gains[:, columns(plane, r)]
+    swap_pass("x")
+    place_rows(plane, core, near_x, far_x, full)
+    for i in range(length // BLOCK):
+        span = slice(i * BLOCK, (i + 1) * BLOCK)
+        x = full[span, :].astype(F32)
+        scale = lax.rsqrt(jnp.mean(x * x, axis=1, keepdims=True) + NORM_EPSILON)
+        value = x * scale * gains_here[0:1, :]
+        normed[span, :] = value.astype(BF16)
+        normed_t[:, span] = value.T.astype(BF16)
+    swap_rows("g", cot, near_g, far_g)
+
+    def head(k, h):
+        at = 2 * k + h
+        lane = pair_lane(length)
+        mine = (lane // HEAD_DIM) == h
+        side = dot(cells[...], layout[at])
+        queries[:, :HALF] = jnp.where(mine, qkv[k, :, :HALF].astype(F32), side[:, :HALF]).astype(BF16)
+        block = lax.broadcasted_iota(jnp.int32, (length, HALF), 0) // HALF
+        is_left, is_right = lane % 8 < block - 1, lane % 8 > block + 1
+        left, right = near[at, :, 0:1], near[at, :, 4 * HALF - 1 :]
+        left_high, right_high = left.astype(BF16).astype(F32), right.astype(BF16).astype(F32)
+        high = jnp.where(is_left, left_high, jnp.where(is_right, right_high, 0.0))
+        low = jnp.where(is_left, left - left_high, jnp.where(is_right, right - right_high, 0.0))
+        ends = jnp.where(lane < HEAD_DIM, side[:, HALF:], jnp.where(lane == HEAD_DIM + 16, 1.0, 0.0))
+        ends = jnp.where((lane >= HEAD_DIM) & (lane < HEAD_DIM + 8), high, ends)
+        ends = jnp.where((lane >= HEAD_DIM + 8) & (lane < HEAD_DIM + 16), low, ends)
+        queries[:, HALF:] = ends.astype(BF16)
+        keys[:, :HALF] = jnp.where(
+            mine, qkv[k, :, HALF : 2 * HALF].astype(F32), cells_twice[...].astype(F32)
+        ).astype(BF16)
+        keys[:, HALF:] = cell_tail[...]
+        scores[...] = dot(queries[...], keys[...], NT)
+        spread = jnp.broadcast_to(near[at], (HALF, 4 * HALF))
+        strip = pltpu.roll(spread, 3 * HALF, 1, stride=1, stride_axis=0)[:, : 3 * HALF]
+        count = length // HALF
+        store = pltpu.make_async_copy(prob.at[h], prob_full.at[at], local_sems.at[4 + h])
+        if k > 0:
+            store.wait()
+        for i in range(count):
+            first, last = max(i - 1, 0), min(i + 2, count)
+            part = strip[:, (first - i + 1) * HALF : (last - i + 1) * HALF]
+            span, near_span = slice(i * HALF, (i + 1) * HALF), slice(first * HALF, last * HALF)
+            scores[span, near_span] = scores[span, near_span] + part
+            row = scores[span, :]
+            top = jnp.max(row, axis=1, keepdims=True)
+            prob[h, span, :] = jnp.exp(row - top).astype(BF16)
+        values = jnp.where(mine, qkv[k, :, 2 * HALF :].astype(F32), 1.0).astype(BF16)
+        mixed = dot(prob[h], values)
+        inv = 1.0 / pltpu.roll(mixed, HEAD_DIM, 1)
+        mixed = (mixed * inv).astype(BF16)
+        store.start()
+        if h == 0:
+            context[k] = mixed
+            inverse[k] = inv
+        else:
+            context[k] = jnp.where(mine, mixed.astype(F32), context[k].astype(F32)).astype(BF16)
+            inverse[k] = jnp.where(mine, inv, inverse[k])
+
+    def project(k):
+        if k > 0:
+            load = pltpu.make_async_copy(att_full.at[k], weights, local_sems.at[3])
+            load.start()
+            load.wait()
+        qkv[k] = dot(normed[...], weights[:, HALF:]).astype(BF16)
+        mixed_all[:, k * HALF : (k + 1) * HALF] = weights[:, 0:HALF]
+
+    def after_head(k, h):
+        if (k, h) == (0, 0):
+            att.plane_start(2)
+            att.corner_start(1)
+        if (k, h) == (0, 1):
+            att.plane_start(3)
+            att.corner_start(2)
+            for step in range(1, RING):
+                ffn.ring_start(step)
+        if (k, h) == (1, 0):
+            att.corner_start(3)
+        if (k, h) == (2, 0):
+            swap_pass("g")
+            ffn.plane_start(1)
+        if (k, h) == (3, 0):
+            ffn.plane_start(2)
+            ffn.corner_start(1)
+
+    for k in range(RING):
+        if k > 0:
+            att.finish(k)
+        project(k)
+        if k == 0:
+            att.plane_start(1)
+            load_in.wait()
+            load_out.wait()
+            own_ffn(core, plane, ffn_in_v, ffn_out_v, own_ffn_w)
+        for h in range(2):
+            head(k, h)
+            after_head(k, h)
+
+    for k in range(RING):
+        out_rows[:, k * HALF : (k + 1) * HALF] = context[k]
+    for i in range(length // BLOCK):
+        span = slice(i * BLOCK, (i + 1) * BLOCK)
+        mine_out[span, :] = dot(out_rows[span, :], mixed_all[...], NT).astype(BF16)
+        lines.start(("out", i), mine_out.at[span], other_out.at[span], partner)
+    place_rows(plane, core, near_g, far_g, cot_full)
+    for r in range(PLANES):
+        lanes = slice(r * BLOCK, (r + 1) * BLOCK)
+        cot_t[lanes, :] = cot_full[:, lanes].astype(F32).T.astype(BF16)
+    for i in range(length // BLOCK):
+        span = slice(i * BLOCK, (i + 1) * BLOCK)
+        lines.arrived(("out", i))
+        row = full[span, :].astype(F32) + (
+            mine_out[span, :].astype(F32) + other_out[span, :].astype(F32)
+        )
+        resid[span, :] = row
+        scale = lax.rsqrt(jnp.mean(row * row, axis=1, keepdims=True) + NORM_EPSILON)
+        value = row * scale * gains_here[1:2, :]
+        normed_two[span, :] = value.astype(BF16)
+        normed_two_t[:, span] = value.T.astype(BF16)
+
+    ffn.plane_start(3)
+    ffn.corner_start(2)
+    ffn.finish(1)
+    ffn.corner_start(3)
+    ffn.finish(2)
+    ffn.finish(3)
+    for h in range(2):
+        pltpu.make_async_copy(prob.at[h], prob_full.at[2 * (RING - 1) + h], local_sems.at[4 + h]).wait()
+    swap_sent("x")
+    swap_sent("g")
+    lines.sent(*[name for name in lines.open if name[0] not in ("x", "g")])
+    keep_ffn = pltpu.make_async_copy(own_ffn_w, ffn_full.at[0], local_sems.at[3])
+    keep_ffn.start()
+    keep_ffn.wait()
+
+
+def hot(reach, width):
+    offsets = np.arange(width) - width // 2
+    found = bucket_table(offsets, BUCKETS, reach)[None, :] == np.arange(HALF)[:, None]
+    return jnp.asarray(found.astype(np.float32), BF16)
+
+
+def forward(tokens, cotangent, gains, qkv_w, out_w, ffn_in, ffn_out, position_tables, page_counts, layout_cells):
+    rows = tokens.shape[0]
+    length = 2 * rows
+    features = PLANES * BLOCK
+    tables = position_tables.transpose(0, 2, 1).reshape(12, BUCKETS)
+    tables = jnp.pad(tables, ((0, 4), (0, HALF - BUCKETS)))
+    ints = jnp.concatenate(
+        [
+            layout_cells.reshape(4, length),
+            jnp.broadcast_to(page_counts[:, None], (2, length)),
+            jnp.zeros((2, length), jnp.int32),
+        ]
+    )
+    args = [tokens, cotangent, gains, qkv_w, out_w, ffn_in, ffn_out, tables, ints]
+    args += [hot(REL_REACH, 4 * HALF), hot(CELLS, HALF)]
+    whole = pl.BlockSpec(memory_space=pltpu.VMEM)
+    outside = pl.BlockSpec(memory_space=pl.ANY)
+    outs = [
+        shaped((RING, features, ATT)), shaped((RING, features, FFW)), shaped((2 * RING, length, length)),
+        shaped((length, features)), shaped((2, features), F32), shaped((features, length)),
+        shaped((length, features), F32), shaped((length, features)), shaped((features, length)),
+        shaped((length, features)), shaped((features, length)),
+        shaped((RING, length, 3 * HALF)), shaped((RING, length, HALF)), shaped((RING, length, HALF), F32),
+        shaped((HALF, length)), shaped((length, HALF)), shaped((length, HALF)),
+    ]
+    scratch = [pltpu.VMEM((rows, features), BF16)] * 4 + [
+        pltpu.VMEM(ints.shape, jnp.int32),
+        pltpu.VMEM((RING,) + tables.shape, F32),
+        pltpu.VMEM((6 * RING, HALF), F32),
+        pltpu.VMEM((2 * RING, HALF, 2 * HALF), BF16),
+        pltpu.VMEM((2 * RING, 1, 4 * HALF), F32),
+        pltpu.VMEM((features, FFW), BF16),
+        pltpu.VMEM(ffn_in.shape, BF16),
+        pltpu.VMEM(ffn_out.shape, BF16),
+        pltpu.VMEM((length, features), BF16),
+        pltpu.VMEM((features, ATT), BF16),
+        pltpu.VMEM((length, HALF), BF16),
+        pltpu.VMEM((length, 2 * HALF), BF16),
+        pltpu.VMEM((length, 2 * HALF), BF16),
+        pltpu.VMEM((length, length), F32),
+        pltpu.VMEM((2, length, length), BF16),
+        pltpu.VMEM((features, RING * HALF), BF16),
+        pltpu.VMEM((length, RING * HALF), BF16),
+        pltpu.VMEM((length, features), BF16),
+        pltpu.VMEM((length, features), BF16),
+        pltpu.SemaphoreType.DMA((48,)),
+        pltpu.SemaphoreType.DMA((48,)),
+        pltpu.SemaphoreType.DMA((6,)),
+    ]
+    in_specs = [whole, outside, whole, whole, whole, outside, outside] + [whole] * 4
+    out_specs = [outside] * 3 + [whole] * 14
+    return pl.pallas_call(
+        forward_kernel,
+        out_shape=outs,
+        in_specs=in_specs,
+        out_specs=out_specs,
+        scratch_shapes=scratch,
+        name="forward",
+        cost_estimate=pl.CostEstimate(flops=10**10, bytes_accessed=10**8, transcendentals=0),
+        compiler_params=pltpu.CompilerParams(
+            vmem_limit_bytes=63 * 1024 * 1024, collective_id=0, has_side_effects=True
+        ),
+    )(*args)
+
+
+def gelu_parts(gate):
+    square = gate * gate
+    ratio = math.sqrt(2.0 / math.pi)
+    bend = jnp.tanh(ratio * gate * (1.0 + 0.044715 * square))
+    half_gate = 0.5 * gate
+    value = half_gate + half_gate * bend
+    slope = 0.5 + 0.5 * bend + half_gate * (1.0 - bend * bend) * (
+        ratio * (1.0 + 3.0 * 0.044715 * square)
+    )
+    return value, slope
+
+
+def middle_kernel(
+    normed, normed_t, cot, cot_t, resid, gains_here, ffn_full,
+    grads_full, low, low_t, half_grad, page_out, gain,
+    weights, hidden, grads, total_in, total_out, mine, other, mine_out, other_out,
+    send_sems, recv_sems, local_sems,
+):
+    plane, core, ring = here()
+    partner = device(plane, 1 - core, ring)
+    lines = Lines(send_sems, recv_sems)
+    length = normed.shape[0]
+    rows = length // 2
+    blocks = length // BLOCK
+
+    def load(k):
+        return pltpu.make_async_copy(ffn_full.at[k], weights.at[k % 2], local_sems.at[k % 2])
+
+    def store(k):
+        return pltpu.make_async_copy(grads.at[k % 2], grads_full.at[k], local_sems.at[2 + k % 2])
+
+    load(0).start()
+    greet([partner])
+    for k in range(RING):
+        if k + 1 < RING:
+            load(k + 1).start()
+        load(k).wait()
+        w = weights.at[k % 2]
+        for i in range(blocks):
+            span = slice(i * BLOCK, (i + 1) * BLOCK)
+            both = dot(normed[span, :], w[:, UNITS:])
+            grad_hidden = dot(cot[span, :], w[:, :UNITS])
+            gate, up = both[:, :UNITS], both[:, UNITS:]
+            value, slope = gelu_parts(gate)
+            hidden[span, :UNITS] = (value * up).astype(BF16)
+            hidden[span, UNITS : 2 * UNITS] = (grad_hidden * up * slope).astype(BF16)
+            hidden[span, 2 * UNITS :] = (grad_hidden * value).astype(BF16)
+            part_in = dot(hidden[span, UNITS:], w[:, UNITS:], NT)
+            part_out = dot(hidden[span, :UNITS], w[:, :UNITS], NT)
+            if k > 0:
+                part_in = total_in[span, :] + part_in
+                part_out = total_out[span, :] + part_out
+            if k + 1 < RING:
+                total_in[span, :] = part_in
+                total_out[span, :] = part_out
+            else:
+                mine[span, :] = part_in.astype(BF16)
+                lines.start(("in", i), mine.at[span], other.at[span], partner)
+                mine_out[span, :] = part_out.astype(BF16)
+        if k + 1 == RING:
+            far = pl.ds(pl.multiple_of((1 - core) * rows, rows), rows)
+            lines.start("out", mine_out.at[far], other_out, partner)
+        if k >= 2:
+            store(k - 2).wait()
+        for i in range(2):
+            span = slice(i * 2 * BLOCK, (i + 1) * 2 * BLOCK)
+            grads[k % 2, span, :UNITS] = dot(cot_t[span, :], hidden[:, :UNITS]).astype(BF16)
+            grads[k % 2, span, UNITS:] = dot(normed_t[span, :], hidden[:, UNITS:]).astype(BF16)
+        store(k).start()
+
+    total = jnp.zeros((1, resid.shape[1]), F32)
+    for i in range(blocks):
+        span = slice(i * BLOCK, (i + 1) * BLOCK)
+        lines.arrived(("in", i))
+        row = resid[span, :]
+        grad = mine[span, :].astype(F32) + other[span, :].astype(F32)
+        scale = lax.rsqrt(jnp.mean(row * row, axis=1, keepdims=True) + NORM_EPSILON)
+        weighted = grad * gains_here[1:2, :]
+        center = jnp.mean(row * weighted, axis=1, keepdims=True)
+        value = cot[span, :].astype(F32) + scale * weighted - row * (scale * scale * scale * center)
+        low[span, :] = value.astype(BF16)
+        low_t[:, span] = value.T.astype(BF16)
+        in_half = core == (i * BLOCK) // rows
+        total = total + jnp.where(in_half, jnp.sum(grad * row * scale, axis=0, keepdims=True), 0.0)
+
+        @pl.when(in_half)
+        def _():
+            first = (i * BLOCK) % rows
+            half_grad[first : first + BLOCK, :] = value
+
+    for r in range(PLANES):
+        gain[:, columns(plane, r)] = total[:, r * BLOCK : (r + 1) * BLOCK]
+    lines.arrived("out")
+    for i in range(rows // BLOCK):
+        span = slice(i * BLOCK, (i + 1) * BLOCK)
+        near = pl.ds(pl.multiple_of(core * rows + i * BLOCK, BLOCK), BLOCK)
+        row = resid[near, :] + (mine_out[near, :].astype(F32) + other_out[span, :].astype(F32))
+        for r in range(PLANES):
+            page_out[span, columns(plane, r)] = row[:, r * BLOCK : (r + 1) * BLOCK].astype(BF16)
+    store(RING - 2).wait()
+    store(RING - 1).wait()
+    lines.sent()
+
+
+def middle(normed, normed_t, cot, cot_t, resid, gains_here, ffn_full):
+    length, features = normed.shape
+    rows = length // 2
+    whole = pl.BlockSpec(memory_space=pltpu.VMEM)
+    outside = pl.BlockSpec(memory_space=pl.ANY)
+    return pl.pallas_call(
+        middle_kernel,
+        out_shape=[
+            shaped((RING, features, FFW)), shaped((length, features)), shaped((features, length)),
+            shaped((rows, features), F32), shaped((rows, features)), shaped((1, features), F32),
+        ],
+        in_specs=[whole] * 6 + [outside],
+        out_specs=[outside] + [whole] * 5,
+        scratch_shapes=[
+            pltpu.VMEM((2, features, FFW), BF16),
+            pltpu.VMEM((length, FFW), BF16),
+            pltpu.VMEM((2, features, FFW), BF16),
+            pltpu.VMEM((length, features), F32),
+            pltpu.VMEM((length, features), F32),
+            pltpu.VMEM((length, features), BF16),
+            pltpu.VMEM((length, features), BF16),
+            pltpu.VMEM((length, features), BF16),
+            pltpu.VMEM((rows, features), BF16),
+            pltpu.SemaphoreType.DMA((8,)),
+            pltpu.SemaphoreType.DMA((8,)),
+            pltpu.SemaphoreType.DMA((4,)),
+        ],
+        name="middle",
+        cost_estimate=pl.CostEstimate(flops=27 * 10**9, bytes_accessed=10**8, transcendentals=0),
+        compiler_params=pltpu.CompilerParams(
+            vmem_limit_bytes=63 * 1024 * 1024, collective_id=1, has_side_effects=True
+        ),
+    )(normed, normed_t, cot, cot_t, resid, gains_here, ffn_full)
+
+
+class Scatter:
+    def __init__(self, lines, tag, k, grads, kept, buffers, where):
+        self.lines, self.tag, self.k, self.grads, self.kept = lines, tag, k, grads, kept
+        self.from_x, self.from_y, self.late, self.same, self.cross = buffers
+        self.plane, self.core, self.ring = where
+        self.to_x = device(self.plane ^ 1, self.core, self.ring)
+        self.to_y = device(self.plane ^ 2, self.core, self.ring)
+
+    def name(self, step):
+        return (self.tag, step, self.k)
+
+    def rows(self, r, half):
+        return slice(r * BLOCK + half * HALF, r * BLOCK + (half + 1) * HALF)
+
+    def start(self):
+        k = self.k
+        for step, r, half, target, goal in (
+            ("x1", 3, 0, self.from_x.at[k, 1], self.to_x),
+            ("y1", 3, 1, self.from_y.at[k, 1], self.to_y),
+            ("x0", 1, 0, self.from_x.at[k, 0], self.to_x),
+            ("y0", 2, 1, self.from_y.at[k, 0], self.to_y),
+        ):
+            self.lines.start(self.name(step), self.grads.at[self.rows(r, half)], target, goal)
+
+    def middle(self):
+        k = self.k
+        self.lines.arrived(self.name("x1"), self.name("y1"))
+        for source, r, half, at, goal, step in (
+            (self.from_x, 2, 0, 0, self.to_y, "late0"),
+            (self.from_y, 1, 1, 1, self.to_x, "late1"),
+        ):
+            kept = self.kept(r, half).astype(F32)
+            source[k, 1] = (kept + source[k, 1].astype(F32)).astype(BF16)
+            self.lines.start(self.name(step), source.at[k, 1], self.late.at[k, at], goal)
+
+    def last(self):
+        k, late = self.k, self.late
+        self.lines.arrived(*[self.name(step) for step in ("x0", "y0", "late0", "late1")])
+        upper = self.kept(0, 0).astype(F32) + self.from_x[k, 0].astype(F32) + late[k, 0].astype(F32)
+        lower = self.kept(0, 1).astype(F32) + self.from_y[k, 0].astype(F32) + late[k, 1].astype(F32)
+        late[k, 0] = jnp.where(self.core == 0, upper, lower).astype(BF16)
+        late[k, 1] = jnp.where(self.core == 0, lower, upper).astype(BF16)
+        goal = (self.ring + k) % RING
+        if k > 0:
+            self.lines.start(
+                self.name("same"), late.at[k, 0], self.same.at[k - 1], device(self.plane, self.core, goal)
+            )
+        self.lines.start(
+            self.name("cross"), late.at[k, 1], self.cross.at[k], device(self.plane, 1 - self.core, goal)
+        )
+
+
+def sum_ring(lines, tag, late, same, cross):
+    for k in range(RING):
+        if k > 0:
+            lines.arrived((tag, "same", k))
+        lines.arrived((tag, "cross", k))
+    mine = late[0, 0].astype(F32)
+    for k in range(1, RING):
+        mine = mine + same[k - 1].astype(F32)
+    other = cross[0].astype(F32)
+    for k in range(1, RING):
+        other = other + cross[k].astype(F32)
+    return mine, other
+
+
+def backward_kernel(
+    low, low_t, normed_t, half_grad, full, gains_here, qkv, context, inverse,
+    cells_t, cells_twice, cell_tail, near_hot, cell_hot, gain_two,
+    att_full, prob_full, ffn_grads, page_out,
+    layer_out, tokens_grad, qkv_grad, out_grad, inner_grad, outer_grad, small_out,
+    weights, prob, scaled, scaled_low, keys, dscores, grad_qkv, att_grads, total, mine_half, far_half,
+    other_half, page_low, swapped, ffn_kept,
+    att_x, att_y, att_late, att_same, att_cross, ffn_x, ffn_y, ffn_late, ffn_same, ffn_cross,
+    diag_near, diag_cell, gain_one, small, small_ring, small_plane, small_core,
+    send_sems, recv_sems, local_sems,
+):
+    plane, core, ring = where = here()
+    native = core == ring % 2
+    length = low.shape[0]
+    rows = length // 2
+    count = length // HALF
+    partner = device(plane, 1 - core, ring)
+    swap = device(plane, 1 - core, ring ^ 1)
+    partners = [partner, swap, device(plane ^ 1, core, ring), device(plane ^ 2, core, ring)]
+    for k in range(1, RING):
+        partners += [device(plane, core, (ring + k) % RING), device(plane, 1 - core, (ring + k) % RING)]
+    lines = Lines(send_sems, recv_sems)
+
+    def load_prob(at):
+        return pltpu.make_async_copy(prob_full.at[at], prob.at[at % 2], local_sems.at[at % 2])
+
+    def load_weights(k):
+        return pltpu.make_async_copy(att_full.at[k], weights.at[k % 2], local_sems.at[2 + k % 2])
+
+    def load_kept(k):
+        return [
+            pltpu.make_async_copy(
+                ffn_grads.at[k, first : first + BLOCK],
+                ffn_kept.at[k % 2, at : at + BLOCK],
+                local_sems.at[4 + 2 * (k % 2) + i],
+            )
+            for i, (first, at) in enumerate(((0, 0), (3 * HALF, BLOCK)))
+        ]
+
+    load_prob(0).start()
+    load_prob(1).start()
+    load_weights(0).start()
+    goals = [partner, device(plane ^ 1, core, ring), device(plane ^ 2, core, ring)] + partners[4:]
+    greet(goals)
+
+    def kept_ffn(k):
+        spots = {(0, 0): 0, (0, 1): HALF, (1, 1): BLOCK, (2, 0): BLOCK + HALF}
+        return lambda r, half: ffn_kept[k % 2, spots[r, half] : spots[r, half] + HALF]
+
+    def kept_att(k):
+        def read(r, half):
+            first = r * BLOCK + half * HALF
+            return att_grads[k, first : first + HALF]
+
+        return read
+
+    ffn = [
+        Scatter(lines, "ffn", k, ffn_grads.at[k], kept_ffn(k), (ffn_x, ffn_y, ffn_late, ffn_same, ffn_cross), where)
+        for k in range(RING)
+    ]
+    att = [
+        Scatter(lines, "att", k, att_grads.at[k], kept_att(k), (att_x, att_y, att_late, att_same, att_cross), where)
+        for k in range(RING)
+    ]
+
+    def ffn_start(k):
+        for copy in load_kept(k):
+            copy.start()
+        ffn[k].start()
+
+    def ffn_middle(k):
+        for copy in load_kept(k):
+            copy.wait()
+        ffn[k].middle()
+
+    ffn_start(0)
+    ffn_start(1)
+    lines.make("layer", page_out, layer_out, swap)
+    keep_layer = pltpu.make_async_copy(page_out, layer_out, local_sems.at[8])
+
+    @pl.when(native)
+    def _():
+        keep_layer.start()
+
+    @pl.when(jnp.logical_not(native))
+    def _():
+        lines.open["layer"].start()
+
+    lane = pair_lane(length)
+    row_block = lax.broadcasted_iota(jnp.int32, (length, HALF), 0) // HALF
+    flip_at = lax.broadcasted_iota(jnp.int32, (HALF, HALF), 0)
+    flip_to = lax.broadcasted_iota(jnp.int32, (HALF, HALF), 1)
+    flip = jnp.where(flip_at + flip_to == HALF - 1, 1.0, 0.0).astype(BF16)
+
+    def enter(k):
+        if k + 1 < RING:
+            load_weights(k + 1).start()
+        load_weights(k).wait()
+        grad_context = dot(low[...], weights[k % 2, :, 0:HALF]).astype(BF16).astype(F32)
+        value = grad_context * inverse[k]
+        scaled[...] = value
+        scaled_low[...] = value.astype(BF16)
+
+    def head(k, h):
+        at = 2 * k + h
+        mine = (lane // HEAD_DIM) == h
+        value = scaled[...]
+        delta = -jnp.sum(
+            jnp.where(mine, value * context[k].astype(F32), 0.0), axis=1, keepdims=True
+        )
+        delta_high = delta.astype(BF16).astype(F32)
+        spare = HEAD_DIM * (1 - h)
+        fill = jnp.where(lane == spare + 1, delta - delta_high, 0.0)
+        left = jnp.where(mine, value, jnp.where(lane == spare, delta_high, fill)).astype(BF16)
+        ones = jnp.where((lane == spare) | (lane == spare + 1), 1.0, 0.0)
+        right = jnp.where(mine, qkv[k, :, 2 * HALF :].astype(F32), ones).astype(BF16)
+        load_prob(at).wait()
+        strips = [jnp.zeros((HALF, HALF), F32) for _ in range(3)]
+        for i in range(length // BLOCK):
+            span = slice(i * BLOCK, (i + 1) * BLOCK)
+            dscore = prob[at % 2, span, :].astype(F32) * dot(left[span, :], right, NT)
+            dscores[span, :] = dscore.astype(BF16)
+            for part in range(BLOCK // HALF):
+                for step in range(3):
+                    block = i * (BLOCK // HALF) + part + step - 1
+                    if 0 <= block < count:
+                        strips[step] = strips[step] + dscore[
+                            part * HALF : (part + 1) * HALF, block * HALF : (block + 1) * HALF
+                        ]
+        keys[:, :HALF] = jnp.where(
+            mine, qkv[k, :, HALF : 2 * HALF].astype(F32), cells_twice[...].astype(F32)
+        ).astype(BF16)
+        keys[:, HALF:] = cell_tail[...]
+        grad_left = dot(dscores[...], keys[...])
+        grad_key = dot(dscores[...], qkv[k, :, :HALF], TN)
+        grad_value = dot(prob[at % 2], scaled_low[...], TN)
+        if at + 2 < 2 * RING:
+            load_prob(at + 2).start()
+        for m, new in enumerate((grad_left[:, :HALF], grad_key, grad_value)):
+            lanes = slice(m * HALF, (m + 1) * HALF)
+            if h == 1:
+                new = jnp.where(mine, new, grad_qkv[:, lanes].astype(F32))
+            grad_qkv[:, lanes] = new.astype(BF16)
+
+        skewed = jnp.zeros((HALF, 3 * HALF), F32)
+        strip = jnp.concatenate(strips, axis=1)
+        for part in split_bf16(strip):
+            skewed = skewed + dot(flip, part)
+        skewed = jnp.concatenate([skewed, jnp.zeros((HALF, HALF), F32)], axis=1)
+        sums = jnp.sum(pltpu.roll(skewed, 1, 1, stride=1, stride_axis=0), axis=0, keepdims=True)
+        tail = grad_left[:, HALF:]
+        in_tail = (lane >= HEAD_DIM) & (lane < HEAD_DIM + 8)
+        far_left = jnp.sum(jnp.where(in_tail & (lane % 8 < row_block - 1), tail, 0.0), axis=0, keepdims=True)
+        far_right = jnp.sum(jnp.where(in_tail & (lane % 8 > row_block + 1), tail, 0.0), axis=0, keepdims=True)
+        wide = lax.broadcasted_iota(jnp.int32, (1, 4 * HALF), 1)
+        sums = sums + jnp.where(wide == 0, jnp.sum(far_left, axis=1, keepdims=True), 0.0)
+        sums = sums + jnp.where(wide == 4 * HALF - 1, jnp.sum(far_right, axis=1, keepdims=True), 0.0)
+        diag_near[at : at + 1, :] = sums
+        by_cell = grad_left[:, :HALF]
+        by_cell = jnp.where(mine, pltpu.roll(by_cell, HEAD_DIM, 1), by_cell)
+        for axis, table in enumerate((by_cell, tail)):
+            table_high = table.astype(BF16)
+            rest = (table - table_high.astype(F32)).astype(BF16)
+            side = cells_t[axis * CELLS : (axis + 1) * CELLS, :]
+            grid = dot(side, table_high) + dot(side, rest)
+            cell_lane = lax.broadcasted_iota(jnp.int32, (CELLS, HALF), 1)
+            grid = jnp.where(cell_lane < CELLS, grid, 0.0)
+            grid = pltpu.roll(grid, 1, 1, stride=1, stride_axis=0)
+            row = axis * 2 * RING + at
+            diag_cell[row : row + 1, :] = jnp.sum(grid, axis=0, keepdims=True)
+
+    def leave(k):
+        w = weights[k % 2, :, HALF:]
+        att_grads[k, :, 0:HALF] = dot(low_t[...], context[k]).astype(BF16)
+        att_grads[k, :, HALF:] = dot(normed_t[...], grad_qkv[...]).astype(BF16)
+        for i in range(length // BLOCK):
+            span = slice(i * BLOCK, (i + 1) * BLOCK)
+            part = dot(grad_qkv[span, :], w, NT)
+            total[span, :] = part if k == 0 else total[span, :] + part
+
+    enter(0)
+    head(0, 0)
+    head(0, 1)
+    ffn_middle(0)
+    leave(0)
+    enter(1)
+    head(1, 0)
+    ffn_middle(1)
+    ffn[0].last()
+    ffn_start(2)
+    head(1, 1)
+    leave(1)
+    enter(2)
+    head(2, 0)
+    ffn[1].last()
+    ffn_start(3)
+    head(2, 1)
+    ffn_middle(2)
+    att[0].start()
+    att[1].start()
+    leave(2)
+    enter(3)
+    head(3, 0)
+    ffn[2].last()
+    att[2].start()
+    head(3, 1)
+    ffn_middle(3)
+    leave(3)
+    att[3].start()
+
+    near = pl.ds(pl.multiple_of(core * rows, rows), rows)
+    far = pl.ds(pl.multiple_of((1 - core) * rows, rows), rows)
+    far_half[...] = total[far, :].astype(BF16)
+    lines.start("half", far_half, other_half, partner)
+    mine_half[...] = total[near, :].astype(BF16)
+    att[0].middle()
+    att[1].middle()
+    lines.arrived("half")
+    gain = jnp.zeros((1, full.shape[1]), F32)
+    for i in range(rows // BLOCK):
+        span = slice(i * BLOCK, (i + 1) * BLOCK)
+        x = full[pl.ds(pl.multiple_of(core * rows + i * BLOCK, BLOCK), BLOCK), :].astype(F32)
+        grad = mine_half[span, :].astype(F32) + other_half[span, :].astype(F32)
+        scale = lax.rsqrt(jnp.mean(x * x, axis=1, keepdims=True) + NORM_EPSILON)
+        weighted = grad * gains_here[0:1, :]
+        center = jnp.mean(x * weighted, axis=1, keepdims=True)
+        value = half_grad[span, :] + scale * weighted - x * (scale * scale * scale * center)
+        gain = gain + jnp.sum(grad * x * scale, axis=0, keepdims=True)
+        for r in range(PLANES):
+            block = value[:, r * BLOCK : (r + 1) * BLOCK]
+            tokens_grad[span, columns(plane, r)] = block
+            page_low[span, columns(plane, r)] = block.astype(BF16)
+    for r in range(PLANES):
+        gain_one[:, columns(plane, r)] = gain[:, r * BLOCK : (r + 1) * BLOCK]
+    lines.make("swap", page_low, swapped, swap)
+
+    @pl.when(jnp.logical_not(native))
+    def _():
+        lines.open["swap"].start()
+
+    near_sums = sum(dot(part, near_hot[...], NT) for part in split_bf16(diag_near[...]))
+    cell_sums = sum(dot(part, cell_hot[...], NT) for part in split_bf16(diag_cell[...]))
+    for k in range(RING):
+        small[k, 0:2, :] = near_sums[2 * k : 2 * k + 2, :]
+        for axis in range(2):
+            first = axis * 2 * RING + 2 * k
+            small[k, 2 * axis + 2 : 2 * axis + 4, :] = cell_sums[first : first + 2, :]
+        small[k, 6:8, :] = jnp.zeros((2, HALF), F32)
+        for j in range(8):
+            lanes = slice(j * HALF, (j + 1) * HALF)
+            small[k, 8 + j : 9 + j, :] = gain_one[:, lanes]
+            small[k, 16 + j : 17 + j, :] = gain_two[:, lanes]
+    for k in range(1, RING):
+        lines.start(("small", k), small.at[k], small_ring.at[k], device(plane, core, (ring + k) % RING))
+    ffn[3].last()
+    att[0].last()
+    att[2].middle()
+    att[1].last()
+    att[3].middle()
+    for k in range(1, RING):
+        lines.arrived(("small", k))
+    small_plane[0] = small[0] + (small_ring[1] + (small_ring[2] + small_ring[3]))
+    lines.start("smallx", small_plane.at[0], small_plane.at[1], device(plane ^ 1, core, ring))
+    att[2].last()
+    lines.arrived("smallx")
+    small_plane[2] = small_plane[0] + small_plane[1]
+    lines.start("smally", small_plane.at[2], small_plane.at[3], device(plane ^ 2, core, ring))
+    att[3].last()
+    lines.arrived("smally")
+    small_core[0] = small_plane[2] + small_plane[3]
+    lines.start("smallc", small_core.at[0], small_core.at[1], partner)
+
+    mine, other = sum_ring(lines, "ffn", ffn_late, ffn_same, ffn_cross)
+    rest = inner_grad.shape[2] - UNITS
+    first_core = jnp.where(core == 0, mine, other)
+    second_core = jnp.where(core == 0, other, mine)
+    for m in range(2):
+        at = (m + 1) * UNITS
+        inner_grad[m, :, 0:UNITS] = first_core[:, at : at + UNITS]
+        inner_grad[m, :, UNITS : UNITS + rest] = second_core[:, at : at + rest]
+    outer_grad[0:UNITS, :] = first_core[:, 0:UNITS].T
+    outer_grad[UNITS : UNITS + rest, :] = second_core[:, 0:UNITS].T[0:rest]
+
+    @pl.when(jnp.logical_not(native))
+    def _():
+        lines.arrived("swap")
+        tokens_grad[...] = swapped[...].astype(F32)
+
+    mine, other = sum_ring(lines, "att", att_late, att_same, att_cross)
+    first_core = jnp.where(core == 0, mine, other)
+    second_core = jnp.where(core == 0, other, mine)
+    for m in range(3):
+        lanes = slice((m + 1) * HALF, (m + 2) * HALF)
+        qkv_grad[m, :, 0:HALF] = first_core[:, lanes]
+        qkv_grad[m, :, HALF : 2 * HALF] = second_core[:, lanes]
+    out_grad[0:HALF, :] = first_core[:, 0:HALF].T
+    out_grad[HALF : 2 * HALF, :] = second_core[:, 0:HALF].T
+
+    lines.arrived("smallc")
+    low_core = jnp.where(core == 0, small_core[0], small_core[1])
+    high_core = jnp.where(core == 0, small_core[1], small_core[0])
+    small_out[0] = low_core
+    small_out[1] = high_core
+
+    @pl.when(native)
+    def _():
+        keep_layer.wait()
+
+    @pl.when(jnp.logical_not(native))
+    def _():
+        lines.arrived("layer")
+        lines.sent("layer", "swap")
+
+    lines.sent(*[name for name in lines.open if name not in ("layer", "swap")])
+
+
+def backward(low, low_t, normed_t, half_grad, full, gains_here, qkv, context, inverse, cells_t, cells_twice, cell_tail, gain_two, att_full, prob_full, ffn_grads, page_out, units):
+    length, features = low.shape
+    rows = length // 2
+    whole = pl.BlockSpec(memory_space=pltpu.VMEM)
+    outside = pl.BlockSpec(memory_space=pl.ANY)
+    args = [low, low_t, normed_t, half_grad, full, gains_here, qkv, context, inverse]
+    args += [cells_t, cells_twice, cell_tail, hot(REL_REACH, 4 * HALF), hot(CELLS, HALF), gain_two]
+    args += [att_full, prob_full, ffn_grads, page_out]
+
+    def buffers(width):
+        return [
+            pltpu.VMEM((RING, 2, HALF, width), BF16),
+            pltpu.VMEM((RING, 2, HALF, width), BF16),
+            pltpu.VMEM((RING, 2, HALF, width), BF16),
+            pltpu.VMEM((RING - 1, HALF, width), BF16),
+            pltpu.VMEM((RING, HALF, width), BF16),
+        ]
+
+    return pl.pallas_call(
+        backward_kernel,
+        out_shape=[
+            shaped((rows, features)), shaped((rows, features), F32),
+            shaped((3, HALF, 2 * HALF), F32), shaped((2 * HALF, HALF), F32),
+            shaped((2, HALF, units), F32), shaped((units, HALF), F32), shaped((2, 24, HALF), F32),
+        ],
+        in_specs=[whole] * 15 + [outside] * 4,
+        out_specs=[outside] + [whole] * 6,
+        scratch_shapes=[
+            pltpu.VMEM((2, features, ATT), BF16),
+            pltpu.VMEM((2, length, length), BF16),
+            pltpu.VMEM((length, HALF), F32),
+            pltpu.VMEM((length, HALF), BF16),
+            pltpu.VMEM((length, 2 * HALF), BF16),
+            pltpu.VMEM((length, length), BF16),
+            pltpu.VMEM((length, 3 * HALF), BF16),
+            pltpu.VMEM((RING, features, ATT), BF16),
+            pltpu.VMEM((length, features), F32),
+            pltpu.VMEM((rows, features), BF16),
+            pltpu.VMEM((rows, features), BF16),
+            pltpu.VMEM((rows, features), BF16),
+            pltpu.VMEM((rows, features), BF16),
+            pltpu.VMEM((rows, features), BF16),
+            pltpu.VMEM((2, 2 * BLOCK, FFW), BF16),
+            *buffers(ATT),
+            *buffers(FFW),
+            pltpu.VMEM((2 * RING, 4 * HALF), F32),
+            pltpu.VMEM((4 * RING, HALF), F32),
+            pltpu.VMEM((1, features), F32),
+            pltpu.VMEM((RING, 24, HALF), F32),
+            pltpu.VMEM((RING, 24, HALF), F32),
+            pltpu.VMEM((4, 24, HALF), F32),
+            pltpu.VMEM((2, 24, HALF), F32),
+            pltpu.SemaphoreType.DMA((80,)),
+            pltpu.SemaphoreType.DMA((80,)),
+            pltpu.SemaphoreType.DMA((9,)),
+        ],
+        name="backward",
+        cost_estimate=pl.CostEstimate(flops=3 * 10**10, bytes_accessed=10**8, transcendentals=0),
+        compiler_params=pltpu.CompilerParams(
+            vmem_limit_bytes=63 * 1024 * 1024, collective_id=2, has_side_effects=True
+        ),
+    )(*args)
+
+
+def page_body(
+    tokens,
+    norm_gains,
+    attn_qkv,
+    attn_out,
+    ffn_in,
+    ffn_out,
+    position_tables,
+    page_counts,
+    layout_cells,
+    cotangent,
+):
+    group, ring = lax.axis_index("dp"), lax.axis_index("tensor")
+    (
+        att_full, ffn_full, prob, full, gains_here, normed_one_t, resid, normed_two, normed_two_t,
+        cot, cot_t, qkv, context, inverse, cells_t, cells_twice, cell_tail,
+    ) = forward(
+        tokens, cotangent, norm_gains, attn_qkv, attn_out, ffn_in, ffn_out, position_tables,
+        page_counts, layout_cells,
+    )
+    ffn_grads, low, low_t, half_grad, page_out, gain_two = middle(
+        normed_two, normed_two_t, cot, cot_t, resid, gains_here, ffn_full
+    )
+    layer_out, tokens_grad, qkv_grad, out_grad, inner_grad, outer_grad, small = backward(
+        low, low_t, normed_one_t, half_grad, full, gains_here, qkv, context, inverse, cells_t,
+        cells_twice, cell_tail, gain_two, att_full, prob, ffn_grads, page_out, ffn_in.shape[2],
+    )
+    gains = (small[0, 8:] + small[1, 8:]).reshape(2, 1024)
+    gains_grad = lax.dynamic_slice_in_dim(gains, (group * RING + ring) * 32, 32, axis=1)
+    tables = small[:, 0:6, :BUCKETS].reshape(CORES, 3, 2, BUCKETS).transpose(1, 3, 0, 2)
+    tables = tables.reshape(3, BUCKETS, 2 * CORES)
+    tables_grad = lax.dynamic_slice_in_dim(tables, group * 4, 4, axis=1)
+    return (
+        layer_out,
+        tokens_grad,
+        gains_grad,
+        qkv_grad,
+        out_grad,
+        inner_grad,
+        outer_grad,
+        tables_grad,
+    )
+
+
 def solution(mesh):
     return jax.shard_map(
-        body,
+        page_body if page_plan(mesh) else general_body,
         mesh=mesh,
         in_specs=(
             P(("dp", "tensor"), None),

time: 2270 us -> 367 us (0.16)
  waiting for transfers between devices: 982 us -> 0 us
  local copies, waits for them, and re-layouts: 699 us -> 15.7 us
  matrix products: 404 us -> 0 us
  Pallas kernels: 0 us -> 341 us
  other arithmetic: 142 us -> 1.41 us
    dot_general x53 -> x0, matrix products: 404 us -> none  [the longest x6 116 us: page_scores(): jnp.einsum('ihd,jhd->hij', query, key_rows, preferred_element_type=jnp.fl...]
    reduce_scatter x5 -> x0, waiting for transfers between devices: 375 us -> none  [the longest x2 150 us: forward_core(): lax.psum_scatter(jnp.dot(context, attn_out, preferred_element_type=jnp.fl...]
    all_gather x6 -> x0, waiting for transfers between devices: 345 us -> none  [the longest x2 101 us: forward_core(): gathered_two = lax.all_gather(normed_two, 'tensor', axis=0, tiled=True)]
    pallas_call x0 -> x3, Pallas kernels: none -> 341 us  [the longest x1 148 us: backward(): pl.pallas_call(backward_kernel, out_shape=[shaped((rows, features)), shap...]
    unnamed x21 -> x0, waiting for transfers between devices: 262 us -> none
    while x57 -> x0, local copies, waits for them, and re-layouts: 177 us -> none
    unnamed x73 -> x22, local copies, waits for them, and re-layouts: 189 us -> 13.5 us
    reshape x6 -> x2, local copies, waits for them, and re-layouts: 135 us -> 0.03 us  [the longest x1 0.02 us: forward(): layout_cells.reshape(4, length)]
  transfers between devices with their start and end apart: 16 -> 0, of which waited for: 15 -> 0; matrix products, arithmetic and copies ran while one was open for 15% -> 0% of each run, Pallas kernels for 0% -> 0%
where the time goes in v1:
time: 367 us; the launch traced here: 360 us
  Pallas kernels  341 us (93%)
  local copies, waits for them, and re-layouts  15.7 us (4%)
    pallas_call x1, Pallas kernels, backward(): pl.pallas_call(backward_kernel, out_shape=[shaped((rows, features)), shap...  148 us
    pallas_call x1, Pallas kernels, forward(): pl.pallas_call(forward_kernel, out_shape=outs, in_specs=in_specs, out_spe...  144 us
    pallas_call x1, Pallas kernels, middle(): pl.pallas_call(middle_kernel, out_shape=[shaped((RING, features, FFW)), s...  49.2 us
    unnamed x22, local copies, waits for them, and re-layouts  13.5 us

profile of v1, /device:TPU:0, one launch (start us, length us, event | category | flops | bytes accessed | tf_op | source)
XLA Modules:
  0.0 359.6 jit_solution(6680351586802015092)
XLA Ops:
  0.6 0.0 copy-start.4
  0.6 0.0 copy-start.6
  0.7 0.0 copy-start.5
  0.7 4.6 %copy.25.ffn_in = bf16[2,1024,704]{2,1,0:T(8,128)(2,1)} copy(bf16[2,1024,704]{1,2,0:T(8,128)(2,1)} %param.18) | data formatting | bytes 5767168 | tf_op args[4]
  5.3 0.0 copy-done.4
  5.3 0.1 pad.7.clone
  5.4 0.0 copy-done.6
  5.4 0.1 pad.6.clone
  5.5 0.7 add_add_fusion.ints
  6.2 0.0 copy-done.5
  6.2 0.6 pad.4.tables
  6.8 144.4 %forward.1 = (bf16[4,1024,512]{2,1,0:T(8,128)(2,1)}, bf16[4,1024,1152]{2,1,0:T(8,128)(2,1)}, bf16[8,1024,1024]{2,1,0:T(8,128)(2,1)}, bf16[1024,1024]{1,0:T(8,128...) custom-call(bf16[512,1024]{1,0:T(8,128)(2,1)} %tokens.1, ...), custom_call_target="tpu_custom_call" | custom-call | flops 10000000000 | bytes 100000000 | tf_op jit(solution)/shard_map/forward/pallas_call | solution.py:869
  151.2 49.2 %middle.1 = (bf16[4,1024,1152]{2,1,0:T(8,128)(2,1)}, bf16[1024,1024]{1,0:T(8,128)(2,1)}, bf16[1024,1024]{1,0:T(8,128)(2,1)}, f32[512,1024]{1,0:T(8,128)}, bf16[512,1024]{1,0:T(8,128)(2,1)}, /*index=5*/f32[1,1024]{1,0:T(1,128)}) custom-call(bf16[1024,1024]{1,0:T(8,128)(2,1)} %get-tuple-element.38.normed, bf16[1024,1024]{1,0:T(8,128)(2,1)} %get-tuple-element.39.normed_t, ...), custom_call_target="tpu_custom_call" | custom-call | flops 27000000512 | bytes 100000000 | tf_op jit(solution)/shard_map/middle/pallas_call | solution.py:992
  200.4 147.7 %backward.1 = (bf16[512,1024]{1,0:T(8,128)(2,1)}, f32[512,1024]{1,0:T(8,128)}, f32[3,128,256]{2,1,0:T(8,128)}, f32[256,128]{1,0:T(8,128)}, f32[2,128,704]{2,1,0:...) custom-call(bf16[1024,1024]{1,0:T(8,128)(2,1)} %get-tuple-element.45.low, ...), custom_call_target="tpu_custom_call" | custom-call | flops 30000001024 | bytes 100000000 | tf_op jit(solution)/shard_map/backward/pallas_call | solution.py:1422
  348.1 0.0 copy-start
  348.1 2.4 copy.28
  350.5 0.7 slice.11
  351.2 0.1 constant_dynamic-slice_fusion
  351.3 0.7 copy.29
  352.0 0.7 slice_add_fusion
  352.7 0.6 constant_dynamic-slice_fusion.1
  353.4 2.3 copy.35
  355.6 0.0 copy-done
  355.6 0.0 copy-start.1
  355.6 0.0 copy-start.3
  355.6 1.3 copy.36
  357.0 0.0 copy-done.1
  357.0 0.7 copy.37
  357.7 0.0 copy-done.3
  357.7 0.7 copy.38
  358.4 0.0 copy-done.2
  358.4 0.7 copy.39
  (7 shorter events, 0.1 us)
Async XLA Ops:
  0.6 4.6 %copy-start.4 = (s32[2,2048]{1,0:T(2,128)S(1)}, s32[2,2048]{1,0:T(2,128)}, u32[]{:S(2)}) copy-start(s32[2,2048]{1,0:T(2,128)} %param.22) | copy-start | bytes 49156
  0.6 4.7 %copy-start.6 = (s32[2]{0:T(128)S(1)}, s32[2]{0:T(128)}, u32[]{:S(2)}) copy-start(s32[2]{0:T(128)} %param.21) | copy-start | bytes 28
  0.7 5.5 %copy-start.5 = (f32[3,32,4]{1,2,0:T(4,128)S(1)}, f32[3,32,4]{1,2,0:T(4,128)}, u32[]{:S(2)}) copy-start(f32[3,32,4]{1,2,0:T(4,128)} %param.20) | copy-start | bytes 4612
  348.1 7.5 %copy-start = (f32[512,1024]{1,0:T(8,128)S(1)}, f32[512,1024]{1,0:T(8,128)}, u32[]{:S(2)}) copy-start(f32[512,1024]{1,0:T(8,128)} %get-tuple-element.93) | copy-start | bytes 6291460
  355.6 1.3 copy-start.1
  355.6 2.1 copy-start.3
  355.6 2.7 copy-start.2

commit v2 on v1

--- a/solution.py
+++ b/solution.py
@@ -387,6 +387,8 @@
 CORES = 2
 BLOCK = 256
 HALF = 128
+ORDER = (0, 1, 3, 2)
+SLOT = (0, 1, 1, 0)
 ATT = 512
 UNITS = 384
 FFW = 3 * UNITS
@@ -470,16 +472,50 @@
         self.lines, self.tag, self.own, self.full = lines, tag, own, full
         self.plane, self.core, self.ring = where
 
+    def place(self, ring):
+        return device(self.plane, self.core, ring)
+
     def ring_start(self, k):
         self.lines.start(
             (self.tag, "z", k),
             self.own.at[0:BLOCK],
             self.full.at[k, 0:BLOCK],
-            device(self.plane, self.core, (self.ring + RING - k) % RING),
+            self.place((self.ring + RING - k) % RING),
         )
 
-    def plane_start(self, k):
-        self.lines.arrived((self.tag, "z", k))
+    def ring_forward(self):
+        for name, k, step in (("down", 1, -1), ("up", 3, 1)):
+            self.lines.make(
+                (self.tag, name),
+                self.full.at[k, 0:BLOCK],
+                self.full.at[2, 0:BLOCK],
+                self.place((self.ring + RING + step) % RING),
+            )
+
+        @pl.when((self.ring == 1) | (self.ring == 2))
+        def _():
+            self.lines.open[self.tag, "down"].start()
+            self.lines.open[self.tag, "up"].start()
+
+    def forward_arrived(self):
+        @pl.when(self.ring < 2)
+        def _():
+            self.lines.arrived((self.tag, "down"))
+
+        @pl.when(self.ring >= 2)
+        def _():
+            self.lines.arrived((self.tag, "up"))
+
+    def forward_sent(self):
+        @pl.when((self.ring == 1) | (self.ring == 2))
+        def _():
+            self.lines.sent((self.tag, "down"), (self.tag, "up"))
+
+    def plane_start(self, k, landed=False):
+        if k == 2 and not landed:
+            self.forward_arrived()
+        elif not landed:
+            self.lines.arrived((self.tag, "z", k))
         for name, r in (("x", 1), ("y", 2)):
             self.lines.start(
                 (self.tag, name, k),
@@ -488,9 +524,13 @@
                 device(self.plane ^ r, self.core, self.ring),
             )
 
-    def corner_start(self, k):
+    def plane_arrived(self, k):
+        self.lines.arrived((self.tag, "x", k), (self.tag, "y", k))
+
+    def corner_start(self, k, landed=False):
+        if not landed:
+            self.plane_arrived(k)
         for name, r, half, goal in (("x", 1, 0, 2), ("y", 2, 1, 1)):
-            self.lines.arrived((self.tag, name, k))
             self.lines.start(
                 (self.tag, "corner" + name, k),
                 self.full.at[k, r * BLOCK + half * HALF : r * BLOCK + (half + 1) * HALF],
@@ -512,15 +552,16 @@
 
 
 def own_ffn(core, plane, inner, outer, target):
-    units = inner.shape[2]
+    units = outer.shape[0]
     for which, first, count in ((0, 0, UNITS), (1, UNITS, units - UNITS)):
 
         @pl.when(core == which)
         def _():
             for r in range(PLANES):
                 rows, place = columns(plane, r), slice(r * BLOCK, (r + 1) * BLOCK)
-                parts = [outer[first : first + count, rows].astype(F32).T.astype(BF16)]
-                parts += [inner[m, rows, first : first + count] for m in range(2)]
+                parts = [outer[first : first + count, rows]]
+                parts += [inner[m, first : first + count, rows] for m in range(2)]
+                parts = [part.astype(F32).T.astype(BF16) for part in parts]
                 for m, part in enumerate(parts):
                     target[place, m * UNITS : m * UNITS + count] = part
                     if count < UNITS:
@@ -640,8 +681,6 @@
     ffn = Gather(lines, "ffn", own_ffn_w, ffn_full, where)
     keep_weights.wait()
     att.own = att_full.at[0]
-    for k in range(1, RING):
-        att.ring_start(k)
 
     lines.arrived("ints")
     page = ring // 2
@@ -674,7 +713,14 @@
 
     for r in range(PLANES):
         gains_here[:, r * BLOCK : (r + 1) * BLOCK] = gains[:, columns(plane, r)]
+    load_in.wait()
+    load_out.wait()
+    own_ffn(core, plane, ffn_in_v, ffn_out_v, own_ffn_w)
+    keep_ffn = pltpu.make_async_copy(own_ffn_w, ffn_full.at[0], local_sems.at[0])
+    keep_ffn.start()
     swap_pass("x")
+    att.ring_start(1)
+    att.ring_start(3)
     place_rows(plane, core, near_x, far_x, full)
     for i in range(length // BLOCK):
         span = slice(i * BLOCK, (i + 1) * BLOCK)
@@ -683,7 +729,6 @@
         value = x * scale * gains_here[0:1, :]
         normed[span, :] = value.astype(BF16)
         normed_t[:, span] = value.T.astype(BF16)
-    swap_rows("g", cot, near_g, far_g)
 
     def head(k, h):
         at = 2 * k + h
@@ -742,31 +787,34 @@
 
     def after_head(k, h):
         if (k, h) == (0, 0):
+            att.plane_start(3)
+            att.ring_forward()
+        if (k, h) == (0, 1):
+            att.corner_start(1)
             att.plane_start(2)
-            att.corner_start(1)
-        if (k, h) == (0, 1):
-            att.plane_start(3)
-            att.corner_start(2)
-            for step in range(1, RING):
-                ffn.ring_start(step)
+            ffn.ring_start(1)
+            swap_rows("g", cot, near_g, far_g)
+            att.finish(1)
         if (k, h) == (1, 0):
             att.corner_start(3)
+        if (k, h) == (1, 1):
+            att.corner_start(2)
+            ffn.plane_start(1)
+            ffn.ring_start(3)
+            att.finish(3)
+        if (k, h) == (3, 0):
+            swap_pass("g")
+        if (k, h) == (3, 1):
+            ffn.corner_start(1)
+            att.finish(2)
         if (k, h) == (2, 0):
-            swap_pass("g")
-            ffn.plane_start(1)
-        if (k, h) == (3, 0):
-            ffn.plane_start(2)
-            ffn.corner_start(1)
-
-    for k in range(RING):
-        if k > 0:
-            att.finish(k)
+            ffn.plane_start(3)
+            ffn.ring_forward()
+
+    for k in ORDER:
         project(k)
         if k == 0:
             att.plane_start(1)
-            load_in.wait()
-            load_out.wait()
-            own_ffn(core, plane, ffn_in_v, ffn_out_v, own_ffn_w)
         for h in range(2):
             head(k, h)
             after_head(k, h)
@@ -793,20 +841,23 @@
         normed_two[span, :] = value.astype(BF16)
         normed_two_t[:, span] = value.T.astype(BF16)
 
-    ffn.plane_start(3)
-    ffn.corner_start(2)
     ffn.finish(1)
-    ffn.corner_start(3)
-    ffn.finish(2)
-    ffn.finish(3)
+    ffn.plane_arrived(3)
+    ffn.forward_arrived()
+    keep_ffn.wait()
     for h in range(2):
-        pltpu.make_async_copy(prob.at[h], prob_full.at[2 * (RING - 1) + h], local_sems.at[4 + h]).wait()
+        pltpu.make_async_copy(prob.at[h], prob_full.at[2 * ORDER[-1] + h], local_sems.at[4 + h]).wait()
     swap_sent("x")
     swap_sent("g")
-    lines.sent(*[name for name in lines.open if name[0] not in ("x", "g")])
-    keep_ffn = pltpu.make_async_copy(own_ffn_w, ffn_full.at[0], local_sems.at[3])
-    keep_ffn.start()
-    keep_ffn.wait()
+    att.forward_sent()
+    ffn.forward_sent()
+    lines.sent(
+        *[
+            name
+            for name in lines.open
+            if name[0] not in ("x", "g") and name[1] not in ("down", "up")
+        ]
+    )
 
 
 def hot(reach, width):
@@ -880,6 +931,65 @@
     )(*args)
 
 
+class Scatter:
+    def __init__(self, lines, tag, k, grads, kept, buffers, where):
+        self.lines, self.tag, self.k, self.grads, self.kept = lines, tag, k, grads, kept
+        self.from_x, self.from_y, self.late, self.same, self.cross = buffers
+        self.plane, self.core, self.ring = where
+        self.to_x = device(self.plane ^ 1, self.core, self.ring)
+        self.to_y = device(self.plane ^ 2, self.core, self.ring)
+
+    def name(self, step):
+        return (self.tag, step, self.k)
+
+    def rows(self, r, half):
+        return slice(r * BLOCK + half * HALF, r * BLOCK + (half + 1) * HALF)
+
+    def start(self):
+        k = self.k
+        for step, r, half, target, goal in (
+            ("x1", 3, 0, self.from_x.at[k, 1], self.to_x),
+            ("y1", 3, 1, self.from_y.at[k, 1], self.to_y),
+            ("x0", 1, 0, self.from_x.at[k, 0], self.to_x),
+            ("y0", 2, 1, self.from_y.at[k, 0], self.to_y),
+        ):
+            self.lines.start(self.name(step), self.grads.at[self.rows(r, half)], target, goal)
+
+    def middle(self):
+        k = self.k
+        self.lines.arrived(self.name("x1"), self.name("y1"))
+        for source, r, half, at, goal, step in (
+            (self.from_x, 2, 0, 0, self.to_y, "late0"),
+            (self.from_y, 1, 1, 1, self.to_x, "late1"),
+        ):
+            kept = self.kept(r, half).astype(F32)
+            source[k, 1] = (kept + source[k, 1].astype(F32)).astype(BF16)
+            self.lines.start(self.name(step), source.at[k, 1], self.late.at[k, at], goal)
+
+    def last(self):
+        self.combine()
+        self.hand_over()
+
+    def combine(self):
+        k, late = self.k, self.late
+        self.lines.arrived(*[self.name(step) for step in ("x0", "y0", "late0", "late1")])
+        upper = self.kept(0, 0).astype(F32) + self.from_x[k, 0].astype(F32) + late[k, 0].astype(F32)
+        lower = self.kept(0, 1).astype(F32) + self.from_y[k, 0].astype(F32) + late[k, 1].astype(F32)
+        late[k, 0] = jnp.where(self.core == 0, upper, lower).astype(BF16)
+        late[k, 1] = jnp.where(self.core == 0, lower, upper).astype(BF16)
+
+    def hand_over(self):
+        k, late = self.k, self.late
+        goal = (self.ring + k) % RING
+        if k > 0:
+            self.lines.start(
+                self.name("same"), late.at[k, 0], self.same.at[k - 1], device(self.plane, self.core, goal)
+            )
+        self.lines.start(
+            self.name("cross"), late.at[k, 1], self.cross.at[k], device(self.plane, 1 - self.core, goal)
+        )
+
+
 def gelu_parts(gate):
     square = gate * gate
     ratio = math.sqrt(2.0 / math.pi)
@@ -893,31 +1003,49 @@
 
 
 def middle_kernel(
-    normed, normed_t, cot, cot_t, resid, gains_here, ffn_full,
-    grads_full, low, low_t, half_grad, page_out, gain,
+    normed, normed_t, cot, cot_t, resid, gains_here, ffn_before,
+    ffn_full, grads_full, low, low_t, half_grad, page_out, gain, late,
     weights, hidden, grads, total_in, total_out, mine, other, mine_out, other_out,
+    kept, from_x, from_y,
     send_sems, recv_sems, local_sems,
 ):
-    plane, core, ring = here()
+    plane, core, ring = where = here()
     partner = device(plane, 1 - core, ring)
     lines = Lines(send_sems, recv_sems)
     length = normed.shape[0]
     rows = length // 2
     blocks = length // BLOCK
 
-    def load(k):
-        return pltpu.make_async_copy(ffn_full.at[k], weights.at[k % 2], local_sems.at[k % 2])
+    gather = Gather(lines, "ffn", None, ffn_full, where)
+
+    def load(at):
+        return pltpu.make_async_copy(
+            ffn_full.at[ORDER[at]], weights.at[at % 2], local_sems.at[at % 2]
+        )
 
     def store(k):
-        return pltpu.make_async_copy(grads.at[k % 2], grads_full.at[k], local_sems.at[2 + k % 2])
-
+        return pltpu.make_async_copy(grads, grads_full.at[k], local_sems.at[2])
+
+    loads = [
+        pltpu.make_async_copy(
+            grads_full.at[0, first : first + BLOCK], kept.at[at : at + BLOCK], local_sems.at[3 + i]
+        )
+        for i, (first, at) in enumerate(((0, 0), (3 * HALF, BLOCK)))
+    ]
+    spots = {(0, 0): 0, (0, 1): HALF, (1, 1): BLOCK, (2, 0): BLOCK + HALF}
+    scatter = Scatter(
+        lines, "grads", 0, grads_full.at[0],
+        lambda r, half: kept[spots[r, half] : spots[r, half] + HALF],
+        (from_x, from_y, late, None, None), where,
+    )
     load(0).start()
-    greet([partner])
-    for k in range(RING):
-        if k + 1 < RING:
-            load(k + 1).start()
-        load(k).wait()
-        w = weights.at[k % 2]
+    load(1).start()
+    greet([partner, device(plane ^ 1, core, ring), device(plane ^ 2, core, ring)])
+    gather.corner_start(3, landed=True)
+    gather.plane_start(2, landed=True)
+    for at, k in enumerate(ORDER):
+        load(at).wait()
+        w = weights.at[at % 2]
         for i in range(blocks):
             span = slice(i * BLOCK, (i + 1) * BLOCK)
             both = dot(normed[span, :], w[:, UNITS:])
@@ -929,26 +1057,40 @@
             hidden[span, 2 * UNITS :] = (grad_hidden * value).astype(BF16)
             part_in = dot(hidden[span, UNITS:], w[:, UNITS:], NT)
             part_out = dot(hidden[span, :UNITS], w[:, :UNITS], NT)
-            if k > 0:
+            if at > 0:
                 part_in = total_in[span, :] + part_in
                 part_out = total_out[span, :] + part_out
-            if k + 1 < RING:
+            if at + 1 < RING:
                 total_in[span, :] = part_in
                 total_out[span, :] = part_out
             else:
                 mine[span, :] = part_in.astype(BF16)
                 lines.start(("in", i), mine.at[span], other.at[span], partner)
                 mine_out[span, :] = part_out.astype(BF16)
-        if k + 1 == RING:
+        if at + 1 == RING:
             far = pl.ds(pl.multiple_of((1 - core) * rows, rows), rows)
             lines.start("out", mine_out.at[far], other_out, partner)
-        if k >= 2:
-            store(k - 2).wait()
+        if at > 0:
+            store(ORDER[at - 1]).wait()
+        if at == 1:
+            gather.finish(3)
+            load(2).start()
+            gather.corner_start(2)
+            scatter.start()
+            for copy in loads:
+                copy.start()
+        if at == 2:
+            gather.finish(2)
+            load(3).start()
         for i in range(2):
             span = slice(i * 2 * BLOCK, (i + 1) * 2 * BLOCK)
-            grads[k % 2, span, :UNITS] = dot(cot_t[span, :], hidden[:, :UNITS]).astype(BF16)
-            grads[k % 2, span, UNITS:] = dot(normed_t[span, :], hidden[:, UNITS:]).astype(BF16)
+            grads[span, :UNITS] = dot(cot_t[span, :], hidden[:, :UNITS]).astype(BF16)
+            grads[span, UNITS:] = dot(normed_t[span, :], hidden[:, UNITS:]).astype(BF16)
         store(k).start()
+        if at == 2:
+            for copy in loads:
+                copy.wait()
+            scatter.middle()
 
     total = jnp.zeros((1, resid.shape[1]), F32)
     for i in range(blocks):
@@ -979,8 +1121,8 @@
         row = resid[near, :] + (mine_out[near, :].astype(F32) + other_out[span, :].astype(F32))
         for r in range(PLANES):
             page_out[span, columns(plane, r)] = row[:, r * BLOCK : (r + 1) * BLOCK].astype(BF16)
-    store(RING - 2).wait()
-    store(RING - 1).wait()
+    scatter.combine()
+    store(ORDER[-1]).wait()
     lines.sent()
 
 
@@ -992,24 +1134,30 @@
     return pl.pallas_call(
         middle_kernel,
         out_shape=[
-            shaped((RING, features, FFW)), shaped((length, features)), shaped((features, length)),
+            shaped((RING, features, FFW)), shaped((RING, features, FFW)),
+            shaped((length, features)), shaped((features, length)),
             shaped((rows, features), F32), shaped((rows, features)), shaped((1, features), F32),
+            shaped((1, 2, HALF, FFW)),
         ],
         in_specs=[whole] * 6 + [outside],
-        out_specs=[outside] + [whole] * 5,
+        out_specs=[outside] * 2 + [whole] * 6,
+        input_output_aliases={6: 0},
         scratch_shapes=[
             pltpu.VMEM((2, features, FFW), BF16),
             pltpu.VMEM((length, FFW), BF16),
-            pltpu.VMEM((2, features, FFW), BF16),
+            pltpu.VMEM((features, FFW), BF16),
             pltpu.VMEM((length, features), F32),
             pltpu.VMEM((length, features), F32),
             pltpu.VMEM((length, features), BF16),
             pltpu.VMEM((length, features), BF16),
             pltpu.VMEM((length, features), BF16),
             pltpu.VMEM((rows, features), BF16),
-            pltpu.SemaphoreType.DMA((8,)),
-            pltpu.SemaphoreType.DMA((8,)),
-            pltpu.SemaphoreType.DMA((4,)),
+            pltpu.VMEM((2 * BLOCK, FFW), BF16),
+            pltpu.VMEM((1, 2, HALF, FFW), BF16),
+            pltpu.VMEM((1, 2, HALF, FFW), BF16),
+            pltpu.SemaphoreType.DMA((20,)),
+            pltpu.SemaphoreType.DMA((20,)),
+            pltpu.SemaphoreType.DMA((5,)),
         ],
         name="middle",
         cost_estimate=pl.CostEstimate(flops=27 * 10**9, bytes_accessed=10**8, transcendentals=0),
@@ -1017,58 +1165,6 @@
             vmem_limit_bytes=63 * 1024 * 1024, collective_id=1, has_side_effects=True
         ),
     )(normed, normed_t, cot, cot_t, resid, gains_here, ffn_full)
-
-
-class Scatter:
-    def __init__(self, lines, tag, k, grads, kept, buffers, where):
-        self.lines, self.tag, self.k, self.grads, self.kept = lines, tag, k, grads, kept
-        self.from_x, self.from_y, self.late, self.same, self.cross = buffers
-        self.plane, self.core, self.ring = where
-        self.to_x = device(self.plane ^ 1, self.core, self.ring)
-        self.to_y = device(self.plane ^ 2, self.core, self.ring)
-
-    def name(self, step):
-        return (self.tag, step, self.k)
-
-    def rows(self, r, half):
-        return slice(r * BLOCK + half * HALF, r * BLOCK + (half + 1) * HALF)
-
-    def start(self):
-        k = self.k
-        for step, r, half, target, goal in (
-            ("x1", 3, 0, self.from_x.at[k, 1], self.to_x),
-            ("y1", 3, 1, self.from_y.at[k, 1], self.to_y),
-            ("x0", 1, 0, self.from_x.at[k, 0], self.to_x),
-            ("y0", 2, 1, self.from_y.at[k, 0], self.to_y),
-        ):
-            self.lines.start(self.name(step), self.grads.at[self.rows(r, half)], target, goal)
-
-    def middle(self):
-        k = self.k
-        self.lines.arrived(self.name("x1"), self.name("y1"))
-        for source, r, half, at, goal, step in (
-            (self.from_x, 2, 0, 0, self.to_y, "late0"),
-            (self.from_y, 1, 1, 1, self.to_x, "late1"),
-        ):
-            kept = self.kept(r, half).astype(F32)
-            source[k, 1] = (kept + source[k, 1].astype(F32)).astype(BF16)
-            self.lines.start(self.name(step), source.at[k, 1], self.late.at[k, at], goal)
-
-    def last(self):
-        k, late = self.k, self.late
-        self.lines.arrived(*[self.name(step) for step in ("x0", "y0", "late0", "late1")])
-        upper = self.kept(0, 0).astype(F32) + self.from_x[k, 0].astype(F32) + late[k, 0].astype(F32)
-        lower = self.kept(0, 1).astype(F32) + self.from_y[k, 0].astype(F32) + late[k, 1].astype(F32)
-        late[k, 0] = jnp.where(self.core == 0, upper, lower).astype(BF16)
-        late[k, 1] = jnp.where(self.core == 0, lower, upper).astype(BF16)
-        goal = (self.ring + k) % RING
-        if k > 0:
-            self.lines.start(
-                self.name("same"), late.at[k, 0], self.same.at[k - 1], device(self.plane, self.core, goal)
-            )
-        self.lines.start(
-            self.name("cross"), late.at[k, 1], self.cross.at[k], device(self.plane, 1 - self.core, goal)
-        )
 
 
 def sum_ring(lines, tag, late, same, cross):
@@ -1087,7 +1183,7 @@
 
 def backward_kernel(
     low, low_t, normed_t, half_grad, full, gains_here, qkv, context, inverse,
-    cells_t, cells_twice, cell_tail, near_hot, cell_hot, gain_two,
+    cells_t, cells_twice, cell_tail, near_hot, cell_hot, gain_two, ffn_first,
     att_full, prob_full, ffn_grads, page_out,
     layer_out, tokens_grad, qkv_grad, out_grad, inner_grad, outer_grad, small_out,
     weights, prob, scaled, scaled_low, keys, dscores, grad_qkv, att_grads, total, mine_half, far_half,
@@ -1109,17 +1205,19 @@
     lines = Lines(send_sems, recv_sems)
 
     def load_prob(at):
-        return pltpu.make_async_copy(prob_full.at[at], prob.at[at % 2], local_sems.at[at % 2])
+        head_at = 2 * ORDER[at // 2] + at % 2
+        return pltpu.make_async_copy(prob_full.at[head_at], prob.at[at % 2], local_sems.at[at % 2])
 
     def load_weights(k):
-        return pltpu.make_async_copy(att_full.at[k], weights.at[k % 2], local_sems.at[2 + k % 2])
+        return pltpu.make_async_copy(att_full.at[k], weights.at[SLOT[k]], local_sems.at[2 + SLOT[k]])
 
     def load_kept(k):
+        slot = SLOT[k]
         return [
             pltpu.make_async_copy(
                 ffn_grads.at[k, first : first + BLOCK],
-                ffn_kept.at[k % 2, at : at + BLOCK],
-                local_sems.at[4 + 2 * (k % 2) + i],
+                ffn_kept.at[slot, at : at + BLOCK],
+                local_sems.at[4 + 2 * slot + i],
             )
             for i, (first, at) in enumerate(((0, 0), (3 * HALF, BLOCK)))
         ]
@@ -1132,7 +1230,7 @@
 
     def kept_ffn(k):
         spots = {(0, 0): 0, (0, 1): HALF, (1, 1): BLOCK, (2, 0): BLOCK + HALF}
-        return lambda r, half: ffn_kept[k % 2, spots[r, half] : spots[r, half] + HALF]
+        return lambda r, half: ffn_kept[SLOT[k], spots[r, half] : spots[r, half] + HALF]
 
     def kept_att(k):
         def read(r, half):
@@ -1160,14 +1258,10 @@
             copy.wait()
         ffn[k].middle()
 
-    ffn_start(0)
     ffn_start(1)
+    ffn_late[0] = ffn_first[0]
+    ffn[0].hand_over()
     lines.make("layer", page_out, layer_out, swap)
-    keep_layer = pltpu.make_async_copy(page_out, layer_out, local_sems.at[8])
-
-    @pl.when(native)
-    def _():
-        keep_layer.start()
 
     @pl.when(jnp.logical_not(native))
     def _():
@@ -1180,10 +1274,11 @@
     flip = jnp.where(flip_at + flip_to == HALF - 1, 1.0, 0.0).astype(BF16)
 
     def enter(k):
-        if k + 1 < RING:
-            load_weights(k + 1).start()
+        at = ORDER.index(k)
+        if at + 1 < RING:
+            load_weights(ORDER[at + 1]).start()
         load_weights(k).wait()
-        grad_context = dot(low[...], weights[k % 2, :, 0:HALF]).astype(BF16).astype(F32)
+        grad_context = dot(low[...], weights[SLOT[k], :, 0:HALF]).astype(BF16).astype(F32)
         value = grad_context * inverse[k]
         scaled[...] = value
         scaled_low[...] = value.astype(BF16)
@@ -1201,7 +1296,8 @@
         left = jnp.where(mine, value, jnp.where(lane == spare, delta_high, fill)).astype(BF16)
         ones = jnp.where((lane == spare) | (lane == spare + 1), 1.0, 0.0)
         right = jnp.where(mine, qkv[k, :, 2 * HALF :].astype(F32), ones).astype(BF16)
-        load_prob(at).wait()
+        turn = 2 * ORDER.index(k) + h
+        load_prob(turn).wait()
         strips = [jnp.zeros((HALF, HALF), F32) for _ in range(3)]
         for i in range(length // BLOCK):
             span = slice(i * BLOCK, (i + 1) * BLOCK)
@@ -1221,8 +1317,8 @@
         grad_left = dot(dscores[...], keys[...])
         grad_key = dot(dscores[...], qkv[k, :, :HALF], TN)
         grad_value = dot(prob[at % 2], scaled_low[...], TN)
-        if at + 2 < 2 * RING:
-            load_prob(at + 2).start()
+        if turn + 2 < 2 * RING:
+            load_prob(turn + 2).start()
         for m, new in enumerate((grad_left[:, :HALF], grad_key, grad_value)):
             lanes = slice(m * HALF, (m + 1) * HALF)
             if h == 1:
@@ -1257,9 +1353,11 @@
             diag_cell[row : row + 1, :] = jnp.sum(grid, axis=0, keepdims=True)
 
     def leave(k):
-        w = weights[k % 2, :, HALF:]
+        w = weights[SLOT[k], :, HALF:]
         att_grads[k, :, 0:HALF] = dot(low_t[...], context[k]).astype(BF16)
         att_grads[k, :, HALF:] = dot(normed_t[...], grad_qkv[...]).astype(BF16)
+        if k == ORDER[-1]:
+            att[k].start()
         for i in range(length // BLOCK):
             span = slice(i * BLOCK, (i + 1) * BLOCK)
             part = dot(grad_qkv[span, :], w, NT)
@@ -1268,40 +1366,36 @@
     enter(0)
     head(0, 0)
     head(0, 1)
-    ffn_middle(0)
+    ffn_middle(1)
+    ffn_start(3)
     leave(0)
     enter(1)
     head(1, 0)
-    ffn_middle(1)
-    ffn[0].last()
-    ffn_start(2)
     head(1, 1)
     leave(1)
+    enter(3)
+    head(3, 0)
+    ffn_middle(3)
+    ffn[1].last()
+    ffn_start(2)
+    att[0].start()
+    head(3, 1)
+    leave(3)
     enter(2)
     head(2, 0)
-    ffn[1].last()
-    ffn_start(3)
     head(2, 1)
     ffn_middle(2)
-    att[0].start()
+    att[0].middle()
     att[1].start()
+    ffn[3].last()
+    att[3].start()
     leave(2)
-    enter(3)
-    head(3, 0)
-    ffn[2].last()
-    att[2].start()
-    head(3, 1)
-    ffn_middle(3)
-    leave(3)
-    att[3].start()
 
     near = pl.ds(pl.multiple_of(core * rows, rows), rows)
     far = pl.ds(pl.multiple_of((1 - core) * rows, rows), rows)
     far_half[...] = total[far, :].astype(BF16)
     lines.start("half", far_half, other_half, partner)
     mine_half[...] = total[near, :].astype(BF16)
-    att[0].middle()
-    att[1].middle()
     lines.arrived("half")
     gain = jnp.zeros((1, full.shape[1]), F32)
     for i in range(rows // BLOCK):
@@ -1339,16 +1433,16 @@
             small[k, 16 + j : 17 + j, :] = gain_two[:, lanes]
     for k in range(1, RING):
         lines.start(("small", k), small.at[k], small_ring.at[k], device(plane, core, (ring + k) % RING))
-    ffn[3].last()
+    ffn[2].last()
+    att[1].middle()
     att[0].last()
-    att[2].middle()
-    att[1].last()
     att[3].middle()
     for k in range(1, RING):
         lines.arrived(("small", k))
     small_plane[0] = small[0] + (small_ring[1] + (small_ring[2] + small_ring[3]))
     lines.start("smallx", small_plane.at[0], small_plane.at[1], device(plane ^ 1, core, ring))
-    att[2].last()
+    att[1].last()
+    att[2].middle()
     lines.arrived("smallx")
     small_plane[2] = small_plane[0] + small_plane[1]
     lines.start("smally", small_plane.at[2], small_plane.at[3], device(plane ^ 2, core, ring))
@@ -1356,15 +1450,16 @@
     lines.arrived("smally")
     small_core[0] = small_plane[2] + small_plane[3]
     lines.start("smallc", small_core.at[0], small_core.at[1], partner)
+    att[2].last()
 
     mine, other = sum_ring(lines, "ffn", ffn_late, ffn_same, ffn_cross)
-    rest = inner_grad.shape[2] - UNITS
+    rest = inner_grad.shape[1] - UNITS
     first_core = jnp.where(core == 0, mine, other)
     second_core = jnp.where(core == 0, other, mine)
     for m in range(2):
         at = (m + 1) * UNITS
-        inner_grad[m, :, 0:UNITS] = first_core[:, at : at + UNITS]
-        inner_grad[m, :, UNITS : UNITS + rest] = second_core[:, at : at + rest]
+        inner_grad[m, 0:UNITS, :] = first_core[:, at : at + UNITS].T
+        inner_grad[m, UNITS : UNITS + rest, :] = second_core[:, at : at + UNITS].T[0:rest]
     outer_grad[0:UNITS, :] = first_core[:, 0:UNITS].T
     outer_grad[UNITS : UNITS + rest, :] = second_core[:, 0:UNITS].T[0:rest]
 
@@ -1389,10 +1484,6 @@
     small_out[0] = low_core
     small_out[1] = high_core
 
-    @pl.when(native)
-    def _():
-        keep_layer.wait()
-
     @pl.when(jnp.logical_not(native))
     def _():
         lines.arrived("layer")
@@ -1401,13 +1492,13 @@
     lines.sent(*[name for name in lines.open if name not in ("layer", "swap")])
 
 
-def backward(low, low_t, normed_t, half_grad, full, gains_here, qkv, context, inverse, cells_t, cells_twice, cell_tail, gain_two, att_full, prob_full, ffn_grads, page_out, units):
+def backward(low, low_t, normed_t, half_grad, full, gains_here, qkv, context, inverse, cells_t, cells_twice, cell_tail, gain_two, ffn_first, att_full, prob_full, ffn_grads, page_out, units):
     length, features = low.shape
     rows = length // 2
     whole = pl.BlockSpec(memory_space=pltpu.VMEM)
     outside = pl.BlockSpec(memory_space=pl.ANY)
     args = [low, low_t, normed_t, half_grad, full, gains_here, qkv, context, inverse]
-    args += [cells_t, cells_twice, cell_tail, hot(REL_REACH, 4 * HALF), hot(CELLS, HALF), gain_two]
+    args += [cells_t, cells_twice, cell_tail, hot(REL_REACH, 4 * HALF), hot(CELLS, HALF), gain_two, ffn_first]
     args += [att_full, prob_full, ffn_grads, page_out]
 
     def buffers(width):
@@ -1424,9 +1515,9 @@
         out_shape=[
             shaped((rows, features)), shaped((rows, features), F32),
             shaped((3, HALF, 2 * HALF), F32), shaped((2 * HALF, HALF), F32),
-            shaped((2, HALF, units), F32), shaped((units, HALF), F32), shaped((2, 24, HALF), F32),
+            shaped((2, units, HALF), F32), shaped((units, HALF), F32), shaped((2, 24, HALF), F32),
         ],
-        in_specs=[whole] * 15 + [outside] * 4,
+        in_specs=[whole] * 16 + [outside] * 4,
         out_specs=[outside] + [whole] * 6,
         scratch_shapes=[
             pltpu.VMEM((2, features, ATT), BF16),
@@ -1482,16 +1573,17 @@
         att_full, ffn_full, prob, full, gains_here, normed_one_t, resid, normed_two, normed_two_t,
         cot, cot_t, qkv, context, inverse, cells_t, cells_twice, cell_tail,
     ) = forward(
-        tokens, cotangent, norm_gains, attn_qkv, attn_out, ffn_in, ffn_out, position_tables,
+        tokens, cotangent, norm_gains, attn_qkv, attn_out, ffn_in.transpose(0, 2, 1), ffn_out, position_tables,
         page_counts, layout_cells,
     )
-    ffn_grads, low, low_t, half_grad, page_out, gain_two = middle(
+    _, ffn_grads, low, low_t, half_grad, page_out, gain_two, ffn_first = middle(
         normed_two, normed_two_t, cot, cot_t, resid, gains_here, ffn_full
     )
-    layer_out, tokens_grad, qkv_grad, out_grad, inner_grad, outer_grad, small = backward(
+    page_got, tokens_grad, qkv_grad, out_grad, inner_grad, outer_grad, small = backward(
         low, low_t, normed_one_t, half_grad, full, gains_here, qkv, context, inverse, cells_t,
-        cells_twice, cell_tail, gain_two, att_full, prob, ffn_grads, page_out, ffn_in.shape[2],
-    )
+        cells_twice, cell_tail, gain_two, ffn_first, att_full, prob, ffn_grads, page_out, ffn_in.shape[2],
+    )
+    layer_out = jnp.where(group % CORES == ring % 2, page_out, page_got)
     gains = (small[0, 8:] + small[1, 8:]).reshape(2, 1024)
     gains_grad = lax.dynamic_slice_in_dim(gains, (group * RING + ring) * 32, 32, axis=1)
     tables = small[:, 0:6, :BUCKETS].reshape(CORES, 3, 2, BUCKETS).transpose(1, 3, 0, 2)
@@ -1503,7 +1595,7 @@
         gains_grad,
         qkv_grad,
         out_grad,
-        inner_grad,
+        inner_grad.transpose(0, 2, 1),
         outer_grad,
         tables_grad,
     )

time: 367 us -> 314 us (0.86); the launches traced: 360 us -> 311 us
  Pallas kernels: 341 us -> 299 us
  local copies, waits for them, and re-layouts: 15.7 us -> 8.62 us
    pallas_call x1, Pallas kernels: 144 us -> 107 us  [forward(): pl.pallas_call(forward_kernel, out_shape=outs, in_specs=in_specs, out_spe...]
    pallas_call x1, Pallas kernels: 148 us -> 131 us  [backward(): pl.pallas_call(backward_kernel, out_shape=[shaped((rows, features)), shap...]
    pallas_call x1, Pallas kernels: 49.2 us -> 60.3 us  [middle(): pl.pallas_call(middle_kernel, out_shape=[shaped((RING, features, FFW)), s...]
    unnamed x22 -> x18, local copies, waits for them, and re-layouts: 13.5 us -> 5.03 us
where the time goes in v2:
time: 314 us; the launch traced here: 311 us
  Pallas kernels  299 us (95%)
  local copies, waits for them, and re-layouts  8.62 us (3%)
  other arithmetic  3.15 us (1%)
    pallas_call x1, Pallas kernels, backward(): pl.pallas_call(backward_kernel, out_shape=[shaped((rows, features)), shap...  131 us
    pallas_call x1, Pallas kernels, forward(): pl.pallas_call(forward_kernel, out_shape=outs, in_specs=in_specs, out_spe...  107 us
    pallas_call x1, Pallas kernels, middle(): pl.pallas_call(middle_kernel, out_shape=[shaped((RING, features, FFW)), s...  60.3 us

profile of v2, /device:TPU:0, one launch (start us, length us, event | category | flops | bytes accessed | tf_op | source)
XLA Modules:
  0.0 311.4 jit_solution(7690936138770224562)
XLA Ops:
  0.6 0.7 reshape.34
  1.4 0.1 pad.7.clone
  1.5 0.7 pad.6.clone
  2.2 0.7 add_add_fusion.ints
  2.9 0.7 reshape.33
  3.6 0.6 pad.4.tables
  4.2 107.4 %forward.1 = (bf16[4,1024,512]{2,1,0:T(8,128)(2,1)}, bf16[4,1024,1152]{2,1,0:T(8,128)(2,1)}, bf16[8,1024,1024]{2,1,0:T(8,128)(2,1)}, bf16[1024,1024]{1,0:T(8,128...) custom-call(bf16[512,1024]{1,0:T(8,128)(2,1)} %tokens.1, ...), custom_call_target="tpu_custom_call" | custom-call | flops 10000000000 | bytes 100000000 | tf_op jit(solution)/shard_map/forward/pallas_call | solution.py:920
  111.6 60.3 %middle.1 = (bf16[4,1024,1152]{2,1,0:T(8,128)(2,1)}, bf16[4,1024,1152]{2,1,0:T(8,128)(2,1)}, bf16[1024,1024]{1,0:T(8,128)(2,1)}, bf16[1024,1024]{1,0:T(8,128)(2,...) custom-call(bf16[1024,1024]{1,0:T(8,128)(2,1)} %get-tuple-element.39, ...), custom_call_target="tpu_custom_call", output_to_operand_aliasing={{0}: (6, {})} | custom-call | flops 27000000512 | bytes 100000000 | tf_op jit(solution)/shard_map/middle/pallas_call | solution.py:1134
  171.9 131.0 %backward.1 = (bf16[512,1024]{1,0:T(8,128)(2,1)}, f32[512,1024]{1,0:T(8,128)}, f32[3,128,256]{2,1,0:T(8,128)}, f32[256,128]{1,0:T(8,128)}, f32[2,704,128]{2,1,0:...) custom-call(bf16[1024,1024]{1,0:T(8,128)(2,1)} %get-tuple-element.47.low, ...), custom_call_target="tpu_custom_call" | custom-call | flops 30000001024 | bytes 100000000 | tf_op jit(solution)/shard_map/backward/pallas_call | solution.py:1513
  302.8 0.0 copy-start.5
  302.9 0.0 copy-start
  302.9 2.5 broadcast_select_fusion
  305.3 0.0 copy-done.5
  305.4 0.1 constant_dynamic-slice_fusion
  305.4 0.7 copy.26
  306.2 0.6 constant_dynamic-slice_fusion.1
  306.8 0.0 copy-done
  306.8 0.0 copy-start.2
  306.8 0.0 copy-start.4
  306.8 0.0 copy-start.1
  306.8 1.3 copy.33
  308.1 0.0 copy-done.2
  308.1 0.0 copy-start.3
  308.1 0.7 copy.34
  308.9 0.0 copy-done.4
  308.9 0.7 copy.35
  309.5 0.0 copy-done.1
  309.5 0.9 copy.36
  310.4 0.0 copy-done.3
  310.4 0.7 copy.37
  (6 shorter events, 0.0 us)
Async XLA Ops:
  302.8 2.5 copy-start.5
  302.9 3.9 %copy-start = (f32[512,1024]{1,0:T(8,128)S(1)}, f32[512,1024]{1,0:T(8,128)}, u32[]{:S(2)}) copy-start(f32[512,1024]{1,0:T(8,128)} %get-tuple-element.87) | copy-start | bytes 6291460
  306.8 1.3 copy-start.2
  306.8 2.1 copy-start.4
  306.8 2.7 copy-start.1
  308.1 2.3 copy-start.3

commit v3 on v2

--- a/solution.py
+++ b/solution.py
@@ -388,7 +388,9 @@
 BLOCK = 256
 HALF = 128
 ORDER = (0, 1, 3, 2)
-SLOT = (0, 1, 1, 0)
+BACK_ORDER = (2, 1, 3, 0)
+SLOT = (1, 1, 0, 0)
+KEPT_SLOT = (0, 1, 0, 0)
 ATT = 512
 UNITS = 384
 FFW = 3 * UNITS
@@ -1205,14 +1207,14 @@
     lines = Lines(send_sems, recv_sems)
 
     def load_prob(at):
-        head_at = 2 * ORDER[at // 2] + at % 2
+        head_at = 2 * BACK_ORDER[at // 2] + at % 2
         return pltpu.make_async_copy(prob_full.at[head_at], prob.at[at % 2], local_sems.at[at % 2])
 
     def load_weights(k):
         return pltpu.make_async_copy(att_full.at[k], weights.at[SLOT[k]], local_sems.at[2 + SLOT[k]])
 
     def load_kept(k):
-        slot = SLOT[k]
+        slot = KEPT_SLOT[k]
         return [
             pltpu.make_async_copy(
                 ffn_grads.at[k, first : first + BLOCK],
@@ -1224,13 +1226,13 @@
 
     load_prob(0).start()
     load_prob(1).start()
-    load_weights(0).start()
+    load_weights(BACK_ORDER[0]).start()
     goals = [partner, device(plane ^ 1, core, ring), device(plane ^ 2, core, ring)] + partners[4:]
     greet(goals)
 
     def kept_ffn(k):
         spots = {(0, 0): 0, (0, 1): HALF, (1, 1): BLOCK, (2, 0): BLOCK + HALF}
-        return lambda r, half: ffn_kept[SLOT[k], spots[r, half] : spots[r, half] + HALF]
+        return lambda r, half: ffn_kept[KEPT_SLOT[k], spots[r, half] : spots[r, half] + HALF]
 
     def kept_att(k):
         def read(r, half):
@@ -1258,7 +1260,7 @@
             copy.wait()
         ffn[k].middle()
 
-    ffn_start(1)
+    ffn_start(2)
     ffn_late[0] = ffn_first[0]
     ffn[0].hand_over()
     lines.make("layer", page_out, layer_out, swap)
@@ -1274,9 +1276,9 @@
     flip = jnp.where(flip_at + flip_to == HALF - 1, 1.0, 0.0).astype(BF16)
 
     def enter(k):
-        at = ORDER.index(k)
+        at = BACK_ORDER.index(k)
         if at + 1 < RING:
-            load_weights(ORDER[at + 1]).start()
+            load_weights(BACK_ORDER[at + 1]).start()
         load_weights(k).wait()
         grad_context = dot(low[...], weights[SLOT[k], :, 0:HALF]).astype(BF16).astype(F32)
         value = grad_context * inverse[k]
@@ -1296,7 +1298,7 @@
         left = jnp.where(mine, value, jnp.where(lane == spare, delta_high, fill)).astype(BF16)
         ones = jnp.where((lane == spare) | (lane == spare + 1), 1.0, 0.0)
         right = jnp.where(mine, qkv[k, :, 2 * HALF :].astype(F32), ones).astype(BF16)
-        turn = 2 * ORDER.index(k) + h
+        turn = 2 * BACK_ORDER.index(k) + h
         load_prob(turn).wait()
         strips = [jnp.zeros((HALF, HALF), F32) for _ in range(3)]
         for i in range(length // BLOCK):
@@ -1356,40 +1358,41 @@
         w = weights[SLOT[k], :, HALF:]
         att_grads[k, :, 0:HALF] = dot(low_t[...], context[k]).astype(BF16)
         att_grads[k, :, HALF:] = dot(normed_t[...], grad_qkv[...]).astype(BF16)
-        if k == ORDER[-1]:
+        if k == BACK_ORDER[-1]:
             att[k].start()
         for i in range(length // BLOCK):
             span = slice(i * BLOCK, (i + 1) * BLOCK)
             part = dot(grad_qkv[span, :], w, NT)
-            total[span, :] = part if k == 0 else total[span, :] + part
-
-    enter(0)
-    head(0, 0)
-    head(0, 1)
-    ffn_middle(1)
-    ffn_start(3)
-    leave(0)
-    enter(1)
-    head(1, 0)
-    head(1, 1)
-    leave(1)
-    enter(3)
-    head(3, 0)
-    ffn_middle(3)
-    ffn[1].last()
-    ffn_start(2)
-    att[0].start()
-    head(3, 1)
-    leave(3)
+            total[span, :] = part if k == BACK_ORDER[0] else total[span, :] + part
+
     enter(2)
     head(2, 0)
     head(2, 1)
     ffn_middle(2)
-    att[0].middle()
+    ffn_start(1)
+    leave(2)
+    enter(1)
+    head(1, 0)
+    ffn[2].last()
+    head(1, 1)
+    leave(1)
+    ffn_middle(1)
+    ffn_start(3)
+    enter(3)
+    head(3, 0)
+    att[2].start()
+    head(3, 1)
+    ffn[1].last()
+    leave(3)
+    enter(0)
+    head(0, 0)
+    ffn_middle(3)
     att[1].start()
+    head(0, 1)
+    att[2].middle()
+    att[3].start()
+    leave(0)
     ffn[3].last()
-    att[3].start()
-    leave(2)
 
     near = pl.ds(pl.multiple_of(core * rows, rows), rows)
     far = pl.ds(pl.multiple_of((1 - core) * rows, rows), rows)
@@ -1433,16 +1436,15 @@
             small[k, 16 + j : 17 + j, :] = gain_two[:, lanes]
     for k in range(1, RING):
         lines.start(("small", k), small.at[k], small_ring.at[k], device(plane, core, (ring + k) % RING))
-    ffn[2].last()
+    att[2].last()
     att[1].middle()
-    att[0].last()
     att[3].middle()
     for k in range(1, RING):
         lines.arrived(("small", k))
     small_plane[0] = small[0] + (small_ring[1] + (small_ring[2] + small_ring[3]))
     lines.start("smallx", small_plane.at[0], small_plane.at[1], device(plane ^ 1, core, ring))
     att[1].last()
-    att[2].middle()
+    att[0].middle()
     lines.arrived("smallx")
     small_plane[2] = small_plane[0] + small_plane[1]
     lines.start("smally", small_plane.at[2], small_plane.at[3], device(plane ^ 2, core, ring))
@@ -1450,7 +1452,7 @@
     lines.arrived("smally")
     small_core[0] = small_plane[2] + small_plane[3]
     lines.start("smallc", small_core.at[0], small_core.at[1], partner)
-    att[2].last()
+    att[0].last()
 
     mine, other = sum_ring(lines, "ffn", ffn_late, ffn_same, ffn_cross)
     rest = inner_grad.shape[1] - UNITS

time: 314 us -> 304 us (0.968)
  Pallas kernels: 299 us -> 289 us
    pallas_call x1, Pallas kernels: 131 us -> 121 us  [backward(): pl.pallas_call(backward_kernel, out_shape=[shaped((rows, features)), shap...]
where the time goes in v3:
time: 304 us; the launch traced here: 301 us
  Pallas kernels  289 us (95%)
  local copies, waits for them, and re-layouts  8.62 us (3%)
  other arithmetic  3.15 us (1%)
    pallas_call x1, Pallas kernels, backward(): pl.pallas_call(backward_kernel, out_shape=[shaped((rows, features)), shap...  121 us
    pallas_call x1, Pallas kernels, forward(): pl.pallas_call(forward_kernel, out_shape=outs, in_specs=in_specs, out_spe...  107 us
    pallas_call x1, Pallas kernels, middle(): pl.pallas_call(middle_kernel, out_shape=[shaped((RING, features, FFW)), s...  60.3 us

profile of v3, /device:TPU:0, one launch (start us, length us, event | category | flops | bytes accessed | tf_op | source)
XLA Modules:
  0.0 301.4 jit_solution(8421810791315179946)
XLA Ops:
  0.6 0.7 reshape.34
  1.4 0.1 pad.7.clone
  1.5 0.7 pad.6.clone
  2.2 0.7 add_add_fusion.ints
  2.9 0.7 reshape.33
  3.6 0.6 pad.4.tables
  4.2 107.4 %forward.1 = (bf16[4,1024,512]{2,1,0:T(8,128)(2,1)}, bf16[4,1024,1152]{2,1,0:T(8,128)(2,1)}, bf16[8,1024,1024]{2,1,0:T(8,128)(2,1)}, bf16[1024,1024]{1,0:T(8,128...) custom-call(bf16[512,1024]{1,0:T(8,128)(2,1)} %tokens.1, ...), custom_call_target="tpu_custom_call" | custom-call | flops 10000000000 | bytes 100000000 | tf_op jit(solution)/shard_map/forward/pallas_call | solution.py:922
  111.6 60.3 %middle.1 = (bf16[4,1024,1152]{2,1,0:T(8,128)(2,1)}, bf16[4,1024,1152]{2,1,0:T(8,128)(2,1)}, bf16[1024,1024]{1,0:T(8,128)(2,1)}, bf16[1024,1024]{1,0:T(8,128)(2,...) custom-call(bf16[1024,1024]{1,0:T(8,128)(2,1)} %get-tuple-element.39, ...), custom_call_target="tpu_custom_call", output_to_operand_aliasing={{0}: (6, {})} | custom-call | flops 27000000512 | bytes 100000000 | tf_op jit(solution)/shard_map/middle/pallas_call | solution.py:1136
  171.9 121.0 %backward.1 = (bf16[512,1024]{1,0:T(8,128)(2,1)}, f32[512,1024]{1,0:T(8,128)}, f32[3,128,256]{2,1,0:T(8,128)}, f32[256,128]{1,0:T(8,128)}, f32[2,704,128]{2,1,0:...) custom-call(bf16[1024,1024]{1,0:T(8,128)(2,1)} %get-tuple-element.47.low, ...), custom_call_target="tpu_custom_call" | custom-call | flops 30000001024 | bytes 100000000 | tf_op jit(solution)/shard_map/backward/pallas_call | solution.py:1515
  292.9 0.0 copy-start.5
  292.9 0.0 copy-start
  292.9 2.5 broadcast_select_fusion
  295.4 0.0 copy-done.5
  295.4 0.1 constant_dynamic-slice_fusion
  295.5 0.7 copy.26
  296.2 0.6 constant_dynamic-slice_fusion.1
  296.8 0.0 copy-done
  296.8 0.0 copy-start.2
  296.8 0.0 copy-start.4
  296.8 0.0 copy-start.1
  296.8 1.3 copy.33
  298.2 0.0 copy-done.2
  298.2 0.0 copy-start.3
  298.2 0.7 copy.34
  298.9 0.0 copy-done.4
  298.9 0.7 copy.35
  299.6 0.0 copy-done.1
  299.6 0.9 copy.36
  300.4 0.0 copy-done.3
  300.4 0.7 copy.37
  (6 shorter events, 0.0 us)
Async XLA Ops:
  292.9 2.5 copy-start.5
  292.9 3.9 %copy-start = (f32[512,1024]{1,0:T(8,128)S(1)}, f32[512,1024]{1,0:T(8,128)}, u32[]{:S(2)}) copy-start(f32[512,1024]{1,0:T(8,128)} %get-tuple-element.87) | copy-start | bytes 6291460
  296.8 1.3 copy-start.2
  296.8 2.1 copy-start.4
  296.8 2.7 copy-start.1
  298.2 2.3 copy-start.3

commit v4 on v3

--- a/solution.py
+++ b/solution.py
@@ -612,10 +612,10 @@
 
 
 def forward_kernel(
-    tokens, cot, gains, qkv_w, out_w, ffn_in, ffn_out, tables, ints, near_hot, cell_hot,
+    tokens, cot, gains, qkv_w, out_w, ffn_in, ffn_out, tables, cell_ids, counts, near_hot, cell_hot,
     att_full, ffn_full, prob_full, full, gains_here, normed_t, resid, normed_two, normed_two_t,
     cot_full, cot_t, qkv, context, inverse, cells_t, cells_twice, cell_tail,
-    near_x, far_x, near_g, far_g, other_ints, table_parts, table_rows, layout, near,
+    near_x, far_x, near_g, far_g, other_ids, other_counts, table_parts, table_rows, layout, near,
     own_ffn_w, ffn_in_v, ffn_out_v, normed, weights, cells, queries, keys, scores, prob,
     mixed_all, out_rows, mine_out, other_out,
     send_sems, recv_sems, local_sems,
@@ -672,7 +672,8 @@
             lines.sent((tag, "give"))
 
     swap_rows("x", tokens, near_x, far_x)
-    lines.start("ints", ints, other_ints, partner)
+    lines.start("ids", cell_ids, other_ids, partner)
+    lines.start("counts", counts, other_counts, partner)
     table_parts[0] = tables[...]
     for k in range(1, RING):
         lines.start(("tables", k), tables, table_parts.at[k], ring_others[k - 1])
@@ -684,13 +685,17 @@
     keep_weights.wait()
     att.own = att_full.at[0]
 
-    lines.arrived("ints")
+    lines.arrived("ids", "counts")
     page = ring // 2
     picked = []
-    for first in (0, 2, 4):
-        own_row = ints[pl.ds(first + page, 1), :]
-        other_row = other_ints[pl.ds(first + page, 1), :]
-        picked.append(jnp.where(native, own_row, other_row))
+    for axis in range(2):
+        span = pl.ds(pl.multiple_of(page * length, length), length)
+        picked.append(
+            jnp.where(native, cell_ids[axis : axis + 1, span], other_ids[axis : axis + 1, span])
+        )
+    picked.append(
+        jnp.where(native, counts[pl.ds(page, 1), :], other_counts[pl.ds(page, 1), :])[:, 0:1]
+    )
     spot = lax.broadcasted_iota(jnp.int32, (CELLS, length), 0)
     cells_x = (jnp.broadcast_to(picked[0], (CELLS, length)) == spot).astype(F32)
     cells_y = (jnp.broadcast_to(picked[1], (CELLS, length)) == spot).astype(F32)
@@ -707,10 +712,11 @@
     cell_tail[...] = jnp.concatenate([cells_y, tail], axis=0).T.astype(BF16)
     for k in range(1, RING):
         lines.arrived(("tables", k))
+    table_rows[...] = jnp.zeros(table_rows.shape, F32)
     for k in range(RING):
         for axis in range(3):
             first = axis * 2 * RING + 2 * k
-            table_rows[first : first + 2, :] = table_parts[k, pl.ds(4 * axis + 2 * core, 2), :]
+            table_rows[first : first + 2, 0:BUCKETS] = table_parts[k, axis, pl.ds(2 * core, 2), :]
     bias_pieces(table_rows[...], near_hot, cell_hot, layout, near)
 
     for r in range(PLANES):
@@ -872,16 +878,9 @@
     rows = tokens.shape[0]
     length = 2 * rows
     features = PLANES * BLOCK
-    tables = position_tables.transpose(0, 2, 1).reshape(12, BUCKETS)
-    tables = jnp.pad(tables, ((0, 4), (0, HALF - BUCKETS)))
-    ints = jnp.concatenate(
-        [
-            layout_cells.reshape(4, length),
-            jnp.broadcast_to(page_counts[:, None], (2, length)),
-            jnp.zeros((2, length), jnp.int32),
-        ]
-    )
-    args = [tokens, cotangent, gains, qkv_w, out_w, ffn_in, ffn_out, tables, ints]
+    tables = position_tables.transpose(0, 2, 1)
+    counts = jnp.broadcast_to(page_counts[:, None], (2, HALF))
+    args = [tokens, cotangent, gains, qkv_w, out_w, ffn_in, ffn_out, tables, layout_cells, counts]
     args += [hot(REL_REACH, 4 * HALF), hot(CELLS, HALF)]
     whole = pl.BlockSpec(memory_space=pltpu.VMEM)
     outside = pl.BlockSpec(memory_space=pl.ANY)
@@ -894,7 +893,8 @@
         shaped((HALF, length)), shaped((length, HALF)), shaped((length, HALF)),
     ]
     scratch = [pltpu.VMEM((rows, features), BF16)] * 4 + [
-        pltpu.VMEM(ints.shape, jnp.int32),
+        pltpu.VMEM(layout_cells.shape, jnp.int32),
+        pltpu.VMEM(counts.shape, jnp.int32),
         pltpu.VMEM((RING,) + tables.shape, F32),
         pltpu.VMEM((6 * RING, HALF), F32),
         pltpu.VMEM((2 * RING, HALF, 2 * HALF), BF16),
@@ -917,7 +917,7 @@
         pltpu.SemaphoreType.DMA((48,)),
         pltpu.SemaphoreType.DMA((6,)),
     ]
-    in_specs = [whole, outside, whole, whole, whole, outside, outside] + [whole] * 4
+    in_specs = [whole, outside, whole, whole, whole, outside, outside] + [whole] * 5
     out_specs = [outside] * 3 + [whole] * 14
     return pl.pallas_call(
         forward_kernel,

time: 304 us -> 302 us (level)
  no operation moved by 1% of the time
where the time goes in v4:
time: 302 us; the launch traced here: 299 us
  Pallas kernels  289 us (96%)
  local copies, waits for them, and re-layouts  7.06 us (2%)
    pallas_call x1, Pallas kernels, backward(): pl.pallas_call(backward_kernel, out_shape=[shaped((rows, features)), shap...  121 us
    pallas_call x1, Pallas kernels, forward(): pl.pallas_call(forward_kernel, out_shape=outs, in_specs=in_specs, out_spe...  107 us
    pallas_call x1, Pallas kernels, middle(): pl.pallas_call(middle_kernel, out_shape=[shaped((RING, features, FFW)), s...  60.4 us

profile of v4, /device:TPU:0, one launch (start us, length us, event | category | flops | bytes accessed | tf_op | source)
XLA Modules:
  0.0 299.3 jit_solution(11312294097944455363)
XLA Ops:
  0.6 1.3 broadcast_in_dim.2.counts
  1.9 107.3 %forward.1 = (bf16[4,1024,512]{2,1,0:T(8,128)(2,1)}, bf16[4,1024,1152]{2,1,0:T(8,128)(2,1)}, bf16[8,1024,1024]{2,1,0:T(8,128)(2,1)}, bf16[1024,1024]{1,0:T(8,128...) custom-call(bf16[512,1024]{1,0:T(8,128)(2,1)} %tokens.1, ...), custom_call_target="tpu_custom_call" | custom-call | flops 10000000000 | bytes 100000000 | tf_op jit(solution)/shard_map/forward/pallas_call | solution.py:922
  109.3 60.4 %middle.1 = (bf16[4,1024,1152]{2,1,0:T(8,128)(2,1)}, bf16[4,1024,1152]{2,1,0:T(8,128)(2,1)}, bf16[1024,1024]{1,0:T(8,128)(2,1)}, bf16[1024,1024]{1,0:T(8,128)(2,...) custom-call(bf16[1024,1024]{1,0:T(8,128)(2,1)} %get-tuple-element.39, ...), custom_call_target="tpu_custom_call", output_to_operand_aliasing={{0}: (6, {})} | custom-call | flops 27000000512 | bytes 100000000 | tf_op jit(solution)/shard_map/middle/pallas_call | solution.py:1136
  169.7 121.0 %backward.1 = (bf16[512,1024]{1,0:T(8,128)(2,1)}, f32[512,1024]{1,0:T(8,128)}, f32[3,128,256]{2,1,0:T(8,128)}, f32[256,128]{1,0:T(8,128)}, f32[2,704,128]{2,1,0:...) custom-call(bf16[1024,1024]{1,0:T(8,128)(2,1)} %get-tuple-element.47.low, ...), custom_call_target="tpu_custom_call" | custom-call | flops 30000001024 | bytes 100000000 | tf_op jit(solution)/shard_map/backward/pallas_call | solution.py:1515
  290.7 0.0 copy-start.5
  290.7 0.0 copy-start
  290.8 2.5 broadcast_select_fusion
  293.2 0.0 copy-done.5
  293.2 0.1 constant_dynamic-slice_fusion
  293.3 0.7 copy.26
  294.0 0.6 constant_dynamic-slice_fusion.1
  294.7 0.0 copy-done
  294.7 0.0 copy-start.2
  294.7 0.0 copy-start.4
  294.7 0.0 copy-start.1
  294.7 1.3 copy.33
  296.0 0.0 copy-done.2
  296.0 0.0 copy-start.3
  296.0 0.7 copy.34
  296.8 0.0 copy-done.4
  296.8 0.7 copy.35
  297.4 0.0 copy-done.1
  297.4 0.9 copy.36
  298.3 0.0 copy-done.3
  298.3 0.7 copy.37
  (5 shorter events, 0.0 us)
Async XLA Ops:
  290.7 2.5 copy-start.5
  290.7 3.9 %copy-start = (f32[512,1024]{1,0:T(8,128)S(1)}, f32[512,1024]{1,0:T(8,128)}, u32[]{:S(2)}) copy-start(f32[512,1024]{1,0:T(8,128)} %get-tuple-element.87) | copy-start | bytes 6291460
  294.7 1.3 copy-start.2
  294.7 2.1 copy-start.4
  294.7 2.7 copy-start.1
  296.0 2.3 copy-start.3

commit v5 on v4

--- a/solution.py
+++ b/solution.py
@@ -387,6 +387,7 @@
 CORES = 2
 BLOCK = 256
 HALF = 128
+PARTS = 2
 ORDER = (0, 1, 3, 2)
 BACK_ORDER = (2, 1, 3, 0)
 SLOT = (1, 1, 0, 0)
@@ -636,40 +637,49 @@
     greet([partner, swap] + ring_others + neighbours)
 
     def swap_rows(tag, source, near_rows, far_rows):
-        lines.make((tag, "swap"), source, near_rows, swap)
-        lines.make((tag, "give"), source, far_rows, partner)
-        lines.make((tag, "pass"), near_rows, far_rows, partner)
+        for part in range(PARTS):
+            span = pl.ds(part * (rows // PARTS), rows // PARTS)
+            lines.make((tag, "swap", part), source.at[span], near_rows.at[span], swap)
+            lines.make((tag, "give", part), source.at[span], far_rows.at[span], partner)
+            lines.make((tag, "pass", part), near_rows.at[span], far_rows.at[span], partner)
 
         @pl.when(native)
         def _():
-            lines.open[tag, "give"].start()
+            for part in range(PARTS):
+                lines.open[tag, "give", part].start()
             keep = pltpu.make_async_copy(source, near_rows, local_sems.at[2])
             keep.start()
             keep.wait()
 
         @pl.when(jnp.logical_not(native))
         def _():
-            lines.open[tag, "swap"].start()
+            for part in range(PARTS):
+                lines.open[tag, "swap", part].start()
 
     def swap_pass(tag):
         @pl.when(jnp.logical_not(native))
         def _():
-            lines.arrived((tag, "swap"))
-            lines.open[tag, "pass"].start()
-            lines.arrived((tag, "give"))
+            for part in range(PARTS):
+                lines.arrived((tag, "swap", part))
+                lines.open[tag, "pass", part].start()
+            for part in range(PARTS):
+                lines.arrived((tag, "give", part))
 
         @pl.when(native)
         def _():
-            lines.arrived((tag, "pass"))
+            for part in range(PARTS):
+                lines.arrived((tag, "pass", part))
 
     def swap_sent(tag):
         @pl.when(jnp.logical_not(native))
         def _():
-            lines.sent((tag, "swap"), (tag, "pass"))
+            for part in range(PARTS):
+                lines.sent((tag, "swap", part), (tag, "pass", part))
 
         @pl.when(native)
         def _():
-            lines.sent((tag, "give"))
+            for part in range(PARTS):
+                lines.sent((tag, "give", part))
 
     swap_rows("x", tokens, near_x, far_x)
     lines.start("ids", cell_ids, other_ids, partner)
@@ -913,8 +923,8 @@
         pltpu.VMEM((length, RING * HALF), BF16),
         pltpu.VMEM((length, features), BF16),
         pltpu.VMEM((length, features), BF16),
-        pltpu.SemaphoreType.DMA((48,)),
-        pltpu.SemaphoreType.DMA((48,)),
+        pltpu.SemaphoreType.DMA((56,)),
+        pltpu.SemaphoreType.DMA((56,)),
         pltpu.SemaphoreType.DMA((6,)),
     ]
     in_specs = [whole, outside, whole, whole, whole, outside, outside] + [whole] * 5
@@ -1414,14 +1424,14 @@
             block = value[:, r * BLOCK : (r + 1) * BLOCK]
             tokens_grad[span, columns(plane, r)] = block
             page_low[span, columns(plane, r)] = block.astype(BF16)
+        lines.make(("swap", i), page_low.at[span], swapped.at[span], swap)
+
+        @pl.when(jnp.logical_not(native))
+        def _():
+            lines.open["swap", i].start()
+
     for r in range(PLANES):
         gain_one[:, columns(plane, r)] = gain[:, r * BLOCK : (r + 1) * BLOCK]
-    lines.make("swap", page_low, swapped, swap)
-
-    @pl.when(jnp.logical_not(native))
-    def _():
-        lines.open["swap"].start()
-
     near_sums = sum(dot(part, near_hot[...], NT) for part in split_bf16(diag_near[...]))
     cell_sums = sum(dot(part, cell_hot[...], NT) for part in split_bf16(diag_cell[...]))
     for k in range(RING):
@@ -1467,7 +1477,7 @@
 
     @pl.when(jnp.logical_not(native))
     def _():
-        lines.arrived("swap")
+        lines.arrived(("swap", 0), ("swap", 1))
         tokens_grad[...] = swapped[...].astype(F32)
 
     mine, other = sum_ring(lines, "att", att_late, att_same, att_cross)
@@ -1489,9 +1499,9 @@
     @pl.when(jnp.logical_not(native))
     def _():
         lines.arrived("layer")
-        lines.sent("layer", "swap")
-
-    lines.sent(*[name for name in lines.open if name not in ("layer", "swap")])
+        lines.sent("layer", ("swap", 0), ("swap", 1))
+
+    lines.sent(*[name for name in lines.open if name != "layer" and name[0] != "swap"])
 
 
 def backward(low, low_t, normed_t, half_grad, full, gains_here, qkv, context, inverse, cells_t, cells_twice, cell_tail, gain_two, ffn_first, att_full, prob_full, ffn_grads, page_out, units):

time: 302 us -> 301 us (level)
  no operation moved by 1% of the time
where the time goes in v5:
time: 301 us; the launch traced here: 299 us
  Pallas kernels  289 us (96%)
  local copies, waits for them, and re-layouts  7.06 us (2%)
    pallas_call x1, Pallas kernels, backward(): pl.pallas_call(backward_kernel, out_shape=[shaped((rows, features)), shap...  121 us
    pallas_call x1, Pallas kernels, forward(): pl.pallas_call(forward_kernel, out_shape=outs, in_specs=in_specs, out_spe...  108 us
    pallas_call x1, Pallas kernels, middle(): pl.pallas_call(middle_kernel, out_shape=[shaped((RING, features, FFW)), s...  59.5 us

profile of v5, /device:TPU:0, one launch (start us, length us, event | category | flops | bytes accessed | tf_op | source)
XLA Modules:
  0.0 299.3 jit_solution(10047462812500623886)
XLA Ops:
  0.6 1.3 broadcast_in_dim.2.counts
  1.9 108.3 %forward.1 = (bf16[4,1024,512]{2,1,0:T(8,128)(2,1)}, bf16[4,1024,1152]{2,1,0:T(8,128)(2,1)}, bf16[8,1024,1024]{2,1,0:T(8,128)(2,1)}, bf16[1024,1024]{1,0:T(8,128...) custom-call(bf16[512,1024]{1,0:T(8,128)(2,1)} %tokens.1, ...), custom_call_target="tpu_custom_call" | custom-call | flops 10000000000 | bytes 100000000 | tf_op jit(solution)/shard_map/forward/pallas_call | solution.py:932
  110.2 59.5 %middle.1 = (bf16[4,1024,1152]{2,1,0:T(8,128)(2,1)}, bf16[4,1024,1152]{2,1,0:T(8,128)(2,1)}, bf16[1024,1024]{1,0:T(8,128)(2,1)}, bf16[1024,1024]{1,0:T(8,128)(2,...) custom-call(bf16[1024,1024]{1,0:T(8,128)(2,1)} %get-tuple-element.39, ...), custom_call_target="tpu_custom_call", output_to_operand_aliasing={{0}: (6, {})} | custom-call | flops 27000000512 | bytes 100000000 | tf_op jit(solution)/shard_map/middle/pallas_call | solution.py:1146
  169.7 121.0 %backward.1 = (bf16[512,1024]{1,0:T(8,128)(2,1)}, f32[512,1024]{1,0:T(8,128)}, f32[3,128,256]{2,1,0:T(8,128)}, f32[256,128]{1,0:T(8,128)}, f32[2,704,128]{2,1,0:...) custom-call(bf16[1024,1024]{1,0:T(8,128)(2,1)} %get-tuple-element.47.low, ...), custom_call_target="tpu_custom_call" | custom-call | flops 30000001024 | bytes 100000000 | tf_op jit(solution)/shard_map/backward/pallas_call | solution.py:1525
  290.7 0.0 copy-start.5
  290.7 0.0 copy-start
  290.7 2.5 broadcast_select_fusion
  293.2 0.0 copy-done.5
  293.2 0.1 constant_dynamic-slice_fusion
  293.3 0.7 copy.26
  294.0 0.6 constant_dynamic-slice_fusion.1
  294.6 0.0 copy-done
  294.6 0.0 copy-start.2
  294.7 0.0 copy-start.4
  294.7 0.0 copy-start.1
  294.7 1.3 copy.33
  296.0 0.0 copy-done.2
  296.0 0.0 copy-start.3
  296.0 0.7 copy.34
  296.7 0.0 copy-done.4
  296.7 0.7 copy.35
  297.4 0.0 copy-done.1
  297.4 0.9 copy.36
  298.3 0.0 copy-done.3
  298.3 0.7 copy.37
  (5 shorter events, 0.0 us)
Async XLA Ops:
  290.7 2.5 copy-start.5
  290.7 3.9 %copy-start = (f32[512,1024]{1,0:T(8,128)S(1)}, f32[512,1024]{1,0:T(8,128)}, u32[]{:S(2)}) copy-start(f32[512,1024]{1,0:T(8,128)} %get-tuple-element.87) | copy-start | bytes 6291460
  294.6 1.3 copy-start.2
  294.7 2.1 copy-start.4
  294.7 2.7 copy-start.1
  296.0 2.3 copy-start.3
